TPU v7x, 128 devices: a whole 4x4x4 slice. The times are simulated.
128 devices in a mesh: ga: 4 (over x), dev: 32 (over z, y, core).
Axes of the slice: x: 4, y: 4, z: 4, core: 2. Of those that a mesh axis runs over, the one named last changes fastest.
Arguments:
- column_state: float32 [6, 72, 65536], P(None, None, ('ga', 'dev')), may hold values from -6 to 6
- neighbours: int32 [16384, 4], P(('ga', 'dev')), may hold values from 0 to 16383, as said below
- crm_slot: int32 [65536], P(('ga', 'dev')), may hold values from 0 to 65535, as said below
- cloudy: int32 [65536], P(('ga', 'dev')), may hold values 0 or 1
- crm_theta: bfloat16 [58, 32, 65536], P(None, None, ('ga', 'dev')), may hold values from -6 to 6
- crm_water: bfloat16 [58, 32, 65536], P(None, None, ('ga', 'dev')), may hold values from -6 to 6
Outputs:
- new_state: float32 [6, 72, 65536], P(None, None, ('ga', 'dev'))
- new_theta: bfloat16 [58, 32, 65536], P(None, None, ('ga', 'dev'))
- new_water: bfloat16 [58, 32, 65536], P(None, None, ('ga', 'dev'))
Inputs may be any that keep to these rules, and one draw needn't show every extreme that they name: Each element's neighbours lie among the elements of the same device, of the device before or of the device after it in the order of ga+dev, wrapping around; each device holds 128 elements in order. crm_slot is a permutation of the slots; slot // 512 is the device that runs the column's cloud model. Every device sends exactly 4 of its columns to every device, and slot % 512 equals the sending device's index times 4 plus the column's rank among those 4.
All inputs are finite; a program needn't handle non-finite values. No bound on the sum of `cloudy` on one device may be relied on, other than what follows from the above.
Results may differ from a plain program's by a relative error of at most 0.001.
Values sent between devices are 32-bit elements; how exact they have to be, the bound alone decides.
A program may use at most 128 MiB of HBM per device.

v0:
```python
import jax
import jax.numpy as jnp
from jax import lax
from jax.sharding import PartitionSpec as P

SUB = 2


DIFFUSION = 0.15
X_DIFFUSION = 0.2
RELAX_RATE = 0.2
LATENT_HEAT = 0.8
STEP_WEIGHT = 0.5


def padded_2(block, sides, width):
    for axis, dim in sides:
        count = lax.axis_size(axis)
        forward = [(i, i + 1) for i in range(count - 1)]
        forward.append((count - 1, 0))
        backward = [(target, source) for source, target in forward]
        low = lax.ppermute(
            lax.slice_in_dim(block, block.shape[dim] - width, None, axis=dim), axis, forward
        )
        high = lax.ppermute(lax.slice_in_dim(block, 0, width, axis=dim), axis, backward)
        block = jnp.concatenate([low, block, high], axis=dim)
    return block


def advect(profile, advection):
    east_side = jnp.roll(profile, -1, axis=1)
    west_side = jnp.roll(profile, 1, axis=1)
    return (
        profile
        - 0.5 * advection * (east_side - west_side)
        + X_DIFFUSION * (east_side - 2.0 * profile + west_side)
    )


def vertical_mix(profile, mixing):
    upper_cell = jnp.concatenate([profile[1:], profile[-1:]], axis=0)
    lower_cell = jnp.concatenate([profile[:1], profile[:-1]], axis=0)
    return profile + mixing * (upper_cell - 2.0 * profile + lower_cell)


def crm_block(large_scale, crm_theta, crm_water, cloudy):
    advection = (0.3 * jnp.tanh(large_scale[0]))[:, None, :]
    mixing = (0.1 + 0.15 * jax.nn.sigmoid(large_scale[1]))[:, None, :]
    target_heat = large_scale[2]
    moisture = large_scale[3]
    target_water = moisture + large_scale[4] + large_scale[5]
    flagged = cloudy.astype(jnp.float32)[None, None, :]
    theta_now = crm_theta.astype(jnp.float32)
    water_now = crm_water.astype(jnp.float32)
    condensed = jnp.zeros_like(theta_now)
    for substep in range(SUB):
        theta_now = vertical_mix(advect(theta_now, advection), mixing)
        water_now = vertical_mix(advect(water_now, advection), mixing)
        theta_now = theta_now + RELAX_RATE * (target_heat - jnp.mean(theta_now, axis=1))[:, None, :]
        water_now = (
            water_now + RELAX_RATE * (target_water - jnp.mean(water_now, axis=1))[:, None, :]
        )
        excess = flagged * 0.5 * jnp.maximum(water_now - 0.5 * theta_now - 0.5, 0.0)
        water_now = water_now - excess
        theta_now = theta_now + LATENT_HEAT * excess
        condensed = condensed + excess
    tendency = jnp.stack(
        [
            jnp.mean(theta_now, axis=1) - target_heat,
            jnp.mean(water_now, axis=1) - moisture,
            jnp.mean(condensed, axis=1) - large_scale[4],
        ]
    )
    return (tendency, theta_now.astype(jnp.bfloat16), water_now.astype(jnp.bfloat16))


def on_device(column_state, neighbours, crm_slot, cloudy, crm_theta, crm_water):
    fields, levels, columns = column_state.shape
    elements = columns // 4
    devices = lax.axis_size(("ga", "dev"))
    crm_levels = crm_theta.shape[0]
    element_mean = jnp.mean(column_state.reshape(fields * levels, elements, 4), axis=-1)
    padded = padded_2(element_mean, ((("ga", "dev"), 1),), elements)
    offset = lax.axis_index(("ga", "dev")) * elements
    relative = (neighbours - offset + elements) % (elements * devices)
    nearby = jnp.sum(jnp.take(padded, relative, axis=1), axis=-1)
    laplace = nearby - 4.0 * element_mean
    dynamics_state = column_state + DIFFUSION * jnp.repeat(laplace, 4, axis=1).reshape(
        fields, levels, columns
    )
    per_peer = columns // devices
    dest_row = crm_slot // columns * per_peer + crm_slot % per_peer
    send_order = (
        jnp.zeros((columns,), jnp.int32).at[dest_row].set(jnp.arange(columns, dtype=jnp.int32))
    )
    low_state = dynamics_state[:, :crm_levels].reshape(fields * crm_levels, columns)
    outgoing = jnp.take(low_state, send_order, axis=1)
    incoming = lax.all_to_all(outgoing, ("ga", "dev"), split_axis=1, concat_axis=1, tiled=True)
    tendency, new_theta, new_water = crm_block(
        incoming.reshape(fields, crm_levels, columns), crm_theta, crm_water, cloudy
    )
    flat_tendency = tendency.reshape(3 * crm_levels, columns)
    returned = lax.all_to_all(flat_tendency, ("ga", "dev"), split_axis=1, concat_axis=1, tiled=True)
    column_tendency = jnp.take(returned, dest_row, axis=1).reshape(3, crm_levels, columns)
    new_state = dynamics_state.at[2:5, :crm_levels].add(STEP_WEIGHT * column_tendency)
    return (new_state, new_theta, new_water)


def solution(mesh):
    return jax.shard_map(
        on_device,
        mesh=mesh,
        in_specs=(
            P(None, None, ("ga", "dev")),
            P(("ga", "dev"), None),
            P(("ga", "dev")),
            P(("ga", "dev")),
            P(None, None, ("ga", "dev")),
            P(None, None, ("ga", "dev")),
        ),
        out_specs=(
            P(None, None, ("ga", "dev")),
            P(None, None, ("ga", "dev")),
            P(None, None, ("ga", "dev")),
        ),
        check_vma=False,
    )
```

profile of v0, /device:TPU:1, one launch (start us, length us, event | category | flops | bytes accessed | tf_op | source)
XLA Modules:
  0.0 206.7 jit_solution(9270474436264895537)
XLA Ops:
  0.7 3.4 %copy.61 = f32[6,72,512]{1,0,2:T(8,128)} copy(f32[6,72,512]{2,1,0:T(8,128)} %param.8) | data formatting | bytes 1769472 | tf_op args[0]
  4.0 2.2 %reshape.187 = f32[432,128,4]{0,2,1:T(4,128)S(1)} reshape(f32[6,72,512]{1,0,2:T(8,128)} %copy.61) | data formatting | bytes 1769472 | tf_op jit(solution)/shard_map/reshape | solution.py:82
  10.3 2.4 %scatter_custom_fusion = s32[512]{0:T(512)S(1)} fusion(s32[512]{0:T(512)S(1)} %get-tuple-element.28, s32[512]{0:T(512)S(1)} %iota.3, s32[]{:T(128)} %constant.148.clone.1), kind=kCustom, calls=%fused_computation.93 | custom fusion | bytes 2052 | tf_op jit(solution)/shard_map/scatter | solution.py:94
  13.3 4.0 %fusion.53 = (f32[58,31,512]{2,1,0:T(8,128)}, f32[58,31,512]{2,1,0:T(8,128)}) fusion(bf16[58,32,512]{2,1,0:T(8,128)(2,1)S(1)} %copy-done.5), kind=kLoop, calls=%fused_computation.113 | loop fusion | bytes 14729216 | tf_op jit(solution)/shard_map/jit(_roll_static)/slice | solution.py:31
  18.2 1.6 gather_fusion
  21.2 2.3 %mul.197 = f32[6,72,512]{1,0,2:T(8,128)} reshape(f32[432,128,4]{0,2,1:T(4,128)S(1)} %broadcast_in_dim.52) | data formatting | bytes 1769472 | tf_op jit(solution)/shard_map/mul | solution.py:88
  23.5 2.5 %add.182 = f32[6,72,512]{1,0,2:T(8,128)S(1)} add(f32[6,72,512]{1,0,2:T(8,128)} %copy.61, f32[6,72,512]{1,0,2:T(8,128)} %mul.197) | non-fusion elementwise | flops 221184 | bytes 2654208 | tf_op jit(solution)/shard_map/add | solution.py:88
  27.3 2.3 %gather_fusion.1 = f32[512,348]{1,0:T(8,128)} fusion(f32[348,512]{0,1:T(8,128)S(1)} %reshape.230, s32[1024]{0:T(1024)S(1)} %pad_clamp_fusion.1), kind=kCustom, calls=%fused_computation.1 | custom fusion | bytes 1427456 | tf_op jit(solution)/shard_map/jit(_take)/gather | solution.py:97
  29.6 1.5 gather.18
  32.2 14.9 %all-to-all-start = ((f32[348,128,4]{0,2,1:T(4,128)}), f32[348,128,4]{0,2,1:T(4,128)S(1)}, u32[]{:S(2)}, u32[]{:S(2)}) async-start(f32[348,128,4]{0,2,1:T(4,128)} %broadcast_select_fusion), calls=%async_computation | async-start | bytes 1572864 | tf_op jit(solution)/shard_map/all_to_all | solution.py:98
  48.0 4.1 %fusion.51 = (f32[58,31,512]{2,1,0:T(8,128)}, f32[58,31,512]{2,1,0:T(8,128)}) fusion(bf16[58,32,512]{2,1,0:T(8,128)(2,1)S(1)} %copy-done.4), kind=kLoop, calls=%fused_computation.111 | loop fusion | bytes 14729216 | tf_op jit(solution)/shard_map/jit(_roll_static)/slice | solution.py:31
  52.1 11.2 %all-to-all-done = f32[348,128,4]{0,2,1:T(4,128)S(1)} async-done(((f32[348,128,4]{0,2,1:T(4,128)}), f32[348,128,4]{0,2,1:T(4,128)S(1)}, u32[]{:S(2)}, u32[]{:S(2)}) %all-to-all-start) | async-done | bytes 712736 | tf_op jit(solution)/shard_map/all_to_all | solution.py:98
  63.3 1.6 fusion.55
  66.0 8.0 %multiply_add_fusion.4 = (f32[58,32,512]{2,1,0:T(8,128)S(1)}, f32[58,32,512]{2,1,0:T(8,128)S(1)}) fusion(f32[58,31,512]{2,1,0:T(8,128)} %get-tuple-element.71, f32[58,1,512]{2,1,0:T(1,128)} %get-tuple-element.73, f32[58,1,512]{2,1,0:T(1,128)} %get-tuple-element.72, f32[58,31,512]{2,1,0:T(8,128)} %get-tuple-element.70, f32[58,512]{1,0:T(8,128)S(1)} %copy.64, ...), kind=kLoop, calls=%fused_computation.35 | loop fusion | flops 20905984 | bytes 26726400 | tf_op jit(solution)/shard_map/add | solution.py:34
  74.0 1.8 copy-done
  77.0 12.8 %fusion.47 = (f32[57,32,512]{2,1,0:T(8,128)}, f32[57,32,512]{2,1,0:T(8,128)}, f32[57,32,512]{2,1,0:T(8,128)}, f32[57,32,512]{2,1,0:T(8,128)}) fusion(f32[58,32,512]{2,1,0:T(8,128)} %copy-done, f32[58,32,512]{2,1,0:T(8,128)} %copy-done.1), kind=kLoop, calls=%fused_computation.107 | loop fusion | bytes 29884416 | tf_op jit(solution)/shard_map/slice | solution.py:41
  90.3 9.5 %fusion.35 = (f32[58,512]{1,0:T(8,128)S(1)}, f32[58,32,512]{2,1,0:T(8,128)S(1)}, f32[58,512]{1,0:T(8,128)S(1)}, f32[58,32,512]{2,1,0:T(8,128)S(1)}) fusion(f32[58,32,512]{2,1,0:T(8,128)} %copy-done, f32[57,32,512]{2,1,0:T(8,128)} %get-tuple-element.63, f32[1,32,512]{2,1,0:T(8,128)S(1)} %get-tuple-element.65, f32[1,32,512]{2,1,0:T(8,128)S(1)} %get-tuple-element.64, ...), kind=kLoop, calls=%fused_computation.97 | loop fusion | flops 15144960 | bytes 30765056 | tf_op jit(solution)/shard_map/reduce_sum | solution.py:61
  99.8 1.9 add_subtract_fusion.1
  103.3 2.8 %fusion.41 = (f32[58,31,512]{2,1,0:T(8,128)S(1)}, f32[58,31,512]{2,1,0:T(8,128)}) fusion(f32[58,32,512]{2,1,0:T(8,128)S(1)} %get-tuple-element.44), kind=kLoop, calls=%fused_computation.101 | loop fusion | bytes 14729216 | tf_op jit(solution)/shard_map/jit(_roll_static)/slice | solution.py:31
  106.3 4.1 %fusion.45 = (f32[58,31,512]{2,1,0:T(8,128)}, f32[58,31,512]{2,1,0:T(8,128)}) fusion(f32[58,32,512]{2,1,0:T(8,128)S(1)} %get-tuple-element.45), kind=kLoop, calls=%fused_computation.105 | loop fusion | bytes 14729216 | tf_op jit(solution)/shard_map/jit(_roll_static)/slice | solution.py:31
  110.4 6.2 %multiply_add_fusion.1 = (f32[58,32,512]{2,1,0:T(8,128)S(1)}, f32[58,32,512]{2,1,0:T(8,128)S(1)}) fusion(f32[58,32,512]{2,1,0:T(8,128)S(1)} %get-tuple-element.44, f32[58,31,512]{2,1,0:T(8,128)} %get-tuple-element.51, f32[58,1,512]{2,1,0:T(1,128)S(1)} %get-tuple-element.53, f32[58,1,512]{2,1,0:T(1,128)S(1)} %get-tuple-element.52, ...), kind=kLoop, calls=%fused_computation.31 | loop fusion | flops 19005440 | bytes 30527488 | tf_op jit(solution)/shard_map/add | solution.py:34
  116.6 4.4 %fusion.39 = (f32[57,32,512]{2,1,0:T(8,128)}, f32[57,32,512]{2,1,0:T(8,128)}) fusion(f32[58,32,512]{2,1,0:T(8,128)S(1)} %get-tuple-element.86), kind=kLoop, calls=%fused_computation.99 | loop fusion | bytes 14942208 | tf_op jit(solution)/shard_map/slice | solution.py:41
  121.8 4.1 %fusion.43 = (f32[57,32,512]{2,1,0:T(8,128)}, f32[57,32,512]{2,1,0:T(8,128)}) fusion(f32[58,32,512]{2,1,0:T(8,128)S(1)} %get-tuple-element.87), kind=kLoop, calls=%fused_computation.103 | loop fusion | bytes 14942208 | tf_op jit(solution)/shard_map/slice | solution.py:41
  126.3 9.6 %fusion.31 = (f32[58,512]{1,0:T(8,128)S(1)}, f32[58,32,512]{2,1,0:T(8,128)S(1)}, f32[58,512]{1,0:T(8,128)S(1)}, f32[58,32,512]{2,1,0:T(8,128)S(1)}) fusion(f32[58,32,512]{2,1,0:T(8,128)} %copy-done.2, f32[57,32,512]{2,1,0:T(8,128)} %get-tuple-element.47, f32[1,32,512]{2,1,0:T(8,128)S(1)} %get-tuple-element.49, f32[1,32,512]{2,1,0:T(8,128)S(1)} %get-tuple-element.48, ...), kind=kLoop, calls=%fused_computation.95 | loop fusion | flops 15144960 | bytes 30765056 | tf_op jit(solution)/shard_map/reduce_sum | solution.py:61
  136.0 6.2 %fusion.12 = (bf16[58,32,512]{2,1,0:T(8,128)(2,1)}, bf16[58,32,512]{2,1,0:T(8,128)(2,1)}, f32[58,512]{1,0:T(8,128)S(1)}, f32[58,512]{1,0:T(8,128)S(1)}, f32[58,512]{1,0:T(8,128)S(1)}) fusion(f32[58,32,512]{2,1,0:T(8,128)S(1)} %get-tuple-element.30, f32[58,512]{1,0:T(8,128)S(1)} %subtract_multiply_fusion, f32[58,32,512]{2,1,0:T(8,128)S(1)} %get-tuple-element.85, ...), kind=kLoop, calls=%fused_computation.39 | loop fusion | flops 21767168 | bytes 19838976 | tf_op jit(solution)/shard_map/convert_element_type | solution.py:74
  144.1 4.8 %all-to-all-start.1 = ((f32[174,128,4]{0,2,1:T(4,128)}), f32[174,128,4]{0,2,1:T(4,128)S(1)}, u32[]{:S(2)}, u32[]{:S(2)}) async-start(f32[174,128,4]{0,2,1:T(4,128)} %all_to_all.13), calls=%async_computation.1 | async-start | bytes 1048576 | tf_op jit(solution)/shard_map/all_to_all | solution.py:103
  148.9 13.5 %all-to-all-done.1 = f32[174,128,4]{0,2,1:T(4,128)S(1)} async-done(((f32[174,128,4]{0,2,1:T(4,128)}), f32[174,128,4]{0,2,1:T(4,128)S(1)}, u32[]{:S(2)}, u32[]{:S(2)}) %all-to-all-start.1) | async-done | bytes 356384 | tf_op jit(solution)/shard_map/all_to_all | solution.py:103
  162.7 1.6 gather_fusion.2
  164.3 1.5 reshape.231
  165.7 3.1 %slice_add_fusion = f32[3,58,512]{1,0,2:T(4,128)S(1)} fusion(f32[6,72,512]{1,0,2:T(8,128)S(1)} %copy-done.11, f32[3,58,512]{1,0,2:T(4,128)} %reshape.231, pred[512]{0:T(512)(128)(4,1)S(1)} %copy-done.19), kind=kLoop, calls=%fused_computation.43 | loop fusion | flops 267264 | bytes 1069568 | tf_op jit(solution)/shard_map/add | solution.py:105
  168.9 36.3 %scatter-add.4 = f32[6,72,512]{1,0,2:T(8,128)S(1)} dynamic-update-slice(f32[6,72,512]{1,0,2:T(8,128)S(1)} %copy-done.11, f32[3,58,512]{1,0,2:T(4,128)S(1)} %slice_add_fusion, s32[]{:T(128)} %constant.172.clone.1, s32[]{:T(128)} %constant.148.clone.1, s32[]{:T(128)} %constant.148.clone.1) | dynamic-update-slice | bytes 712708 | tf_op jit(solution)/shard_map/scatter-add | solution.py:105
  205.2 1.5 copy.76
  (90 shorter events, 18.0 us)
Async XLA Ops:
  0.6 9.0 %copy-start.16 = (s32[512]{0:T(512)S(1)}, s32[512]{0:T(512)}, u32[]{:S(2)}) copy-start(s32[512]{0:T(512)} %param.10) | copy-start | bytes 6148
  0.6 12.3 %copy-start.17 = (s32[128,4]{0,1:T(4,128)S(1)}, s32[128,4]{0,1:T(4,128)}, u32[]{:S(2)}) copy-start(s32[128,4]{0,1:T(4,128)} %param.9) | copy-start | bytes 6148
  0.7 12.7 %copy-start.5 = (bf16[58,32,512]{2,1,0:T(8,128)(2,1)S(1)}, bf16[58,32,512]{2,1,0:T(8,128)(2,1)}, u32[]{:S(2)}) copy-start(bf16[58,32,512]{2,1,0:T(8,128)(2,1)} %param.12) | copy-start | bytes 5701636
  6.8 11.3 %collective-permute-start.1 = (f32[432,128]{0,1:T(8,128)S(1)}, f32[432,128]{0,1:T(8,128)S(1)}, u32[]{:S(2)}, u32[]{:S(2)}) collective-permute-start(f32[432,128]{0,1:T(8,128)S(1)} %broadcast_multiply_fusion), channel_id=1, source_target_pairs={{1,0},{2,1},{3,2},{4,3},{5,4},{6,5},{7,6},{8,7},{9,8},{10,9},{11,1... | collective-permute-start | bytes 663560 | tf_op jit(solution)/shard_map/ppermute | solution.py:25
  8.3 9.9 %collective-permute-start = (f32[432,128]{0,1:T(8,128)S(1)}, f32[432,128]{0,1:T(8,128)S(1)}, u32[]{:S(2)}, u32[]{:S(2)}) collective-permute-start(f32[432,128]{0,1:T(8,128)S(1)} %broadcast_multiply_fusion), channel_id=1, source_target_pairs={{0,1},{1,2},{2,3},{3,4},{4,5},{5,6},{6,7},{7,8},{8,9},{9,10},{10,1... | collective-permute-start | bytes 663560 | tf_op jit(solution)/shard_map/ppermute | solution.py:22
  10.3 2.8 %copy-start.14 = (s32[512]{0:T(512)}, s32[512]{0:T(512)S(1)}, u32[]{:S(2)}) copy-start(s32[512]{0:T(512)S(1)} %get-tuple-element.28) | copy-start | bytes 6148
  26.0 1.3 copy-start.10
  29.6 17.6 %copy-start.18 = (s32[512]{0:T(512)S(1)}, s32[512]{0:T(512)}, u32[]{:S(2)}) copy-start(s32[512]{0:T(512)} %param.11) | copy-start | bytes 6148
  29.6 17.6 %copy-start.4 = (bf16[58,32,512]{2,1,0:T(8,128)(2,1)S(1)}, bf16[58,32,512]{2,1,0:T(8,128)(2,1)}, u32[]{:S(2)}) copy-start(bf16[58,32,512]{2,1,0:T(8,128)(2,1)} %param.13) | copy-start | bytes 5701636
  32.2 31.1 %all-to-all-start = ((f32[348,128,4]{0,2,1:T(4,128)}), f32[348,128,4]{0,2,1:T(4,128)S(1)}, u32[]{:S(2)}, u32[]{:S(2)}) async-start(f32[348,128,4]{0,2,1:T(4,128)} %broadcast_select_fusion), calls=%async_computation | async-start | bytes 1572864 | tf_op jit(solution)/shard_map/all_to_all | solution.py:98
  74.0 1.8 copy-start
  74.0 3.0 %copy-start.1 = (f32[58,32,512]{2,1,0:T(8,128)}, f32[58,32,512]{2,1,0:T(8,128)S(1)}, u32[]{:S(2)}) copy-start(f32[58,32,512]{2,1,0:T(8,128)S(1)} %get-tuple-element.91) | copy-start | bytes 11403268
  77.0 12.8 %copy-start.13 = (f32[58,128,4]{0,2,1:T(4,128)S(1)}, f32[58,128,4]{0,2,1:T(4,128)}, u32[]{:S(2)}) copy-start(f32[58,128,4]{0,2,1:T(4,128)} %get-tuple-element.79) | copy-start | bytes 356356
  77.0 13.0 %copy-start.12 = (f32[58,128,4]{0,2,1:T(4,128)S(1)}, f32[58,128,4]{0,2,1:T(4,128)}, u32[]{:S(2)}) copy-start(f32[58,128,4]{0,2,1:T(4,128)} %get-tuple-element.82) | copy-start | bytes 356356
  99.7 2.5 %copy-start.6 = (f32[58,32,512]{2,1,0:T(8,128)}, f32[58,32,512]{2,1,0:T(8,128)S(1)}, u32[]{:S(2)}) copy-start(f32[58,32,512]{2,1,0:T(8,128)S(1)} %get-tuple-element.34) | copy-start | bytes 11403268
  99.7 3.3 %copy-start.8 = (f32[58,32,512]{2,1,0:T(8,128)}, f32[58,32,512]{2,1,0:T(8,128)S(1)}, u32[]{:S(2)}) copy-start(f32[58,32,512]{2,1,0:T(8,128)S(1)} %get-tuple-element.89) | copy-start | bytes 11403268
  116.6 4.5 %copy-start.2 = (f32[58,32,512]{2,1,0:T(8,128)}, f32[58,32,512]{2,1,0:T(8,128)S(1)}, u32[]{:S(2)}) copy-start(f32[58,32,512]{2,1,0:T(8,128)S(1)} %get-tuple-element.86) | copy-start | bytes 11403268
  116.6 5.2 %copy-start.3 = (f32[58,32,512]{2,1,0:T(8,128)}, f32[58,32,512]{2,1,0:T(8,128)S(1)}, u32[]{:S(2)}) copy-start(f32[58,32,512]{2,1,0:T(8,128)S(1)} %get-tuple-element.87) | copy-start | bytes 11403268
  126.3 9.7 %copy-start.7 = (f32[58,32,512]{2,1,0:T(8,128)S(1)}, f32[58,32,512]{2,1,0:T(8,128)}, u32[]{:S(2)}) copy-start(f32[58,32,512]{2,1,0:T(8,128)} %copy-done.6) | copy-start | bytes 11403268
  126.3 9.7 %copy-start.9 = (f32[58,32,512]{2,1,0:T(8,128)S(1)}, f32[58,32,512]{2,1,0:T(8,128)}, u32[]{:S(2)}) copy-start(f32[58,32,512]{2,1,0:T(8,128)} %copy-done.8) | copy-start | bytes 11403268
  142.2 6.7 %copy-start.15 = (s32[512]{0:T(512)S(1)}, s32[512]{0:T(512)}, u32[]{:S(2)}) copy-start(s32[512]{0:T(512)} %copy-done.14) | copy-start | bytes 6148
  144.1 21.6 %copy-start.11 = (f32[6,72,512]{1,0,2:T(8,128)S(1)}, f32[6,72,512]{1,0,2:T(8,128)}, u32[]{:S(2)}) copy-start(f32[6,72,512]{1,0,2:T(8,128)} %copy-done.10) | copy-start | bytes 2654212
  144.1 21.6 %copy-start.19 = (pred[512]{0:T(512)(128)(4,1)S(1)}, pred[512]{0:T(512)(128)(4,1)}, u32[]{:S(2)}) copy-start(pred[512]{0:T(512)(128)(4,1)} %get-tuple-element.27) | copy-start | bytes 1540
  144.1 18.4 %all-to-all-start.1 = ((f32[174,128,4]{0,2,1:T(4,128)}), f32[174,128,4]{0,2,1:T(4,128)S(1)}, u32[]{:S(2)}, u32[]{:S(2)}) async-start(f32[174,128,4]{0,2,1:T(4,128)} %all_to_all.13), calls=%async_computation.1 | async-start | bytes 1048576 | tf_op jit(solution)/shard_map/all_to_all | solution.py:103
where the time goes:
time: 207 us
  local copies, waits for them, and re-layouts  106 us (51%)
  other arithmetic  52 us (25%)
  waiting for transfers between devices  24.8 us (12%)
  starting transfers between devices  22.5 us (11%)
    scatter-add x1, local copies, waits for them, and re-layouts, on_device(): dynamics_state.at[2:5, :crm_levels].add(STEP_WEIGHT * column_tendency)  36.3 us
    slice x6, local copies, waits for them, and re-layouts, vertical_mix(): upper_cell = jnp.concatenate([profile[1:], profile[-1:]], axis=0)  21.4 us
    reduce_sum x2, other arithmetic, crm_block(): jnp.mean(water_now, axis=1)  19 us
    slice x8, local copies, waits for them, and re-layouts, advect(): east_side = jnp.roll(profile, -1, axis=1)  17.1 us
    all_to_all x1, starting transfers between devices, on_device(): lax.all_to_all(outgoing, ('ga', 'dev'), split_axis=1, concat_axis=1, tile...  14.9 us
    add x2, other arithmetic, advect(): profile - 0.5 * advection * (east_side - west_side)  14.2 us
    all_to_all x1, waiting for transfers between devices, on_device(): lax.all_to_all(flat_tendency, ('ga', 'dev'), split_axis=1, concat_axis=1,...  13.5 us
    all_to_all x1, waiting for transfers between devices, on_device(): lax.all_to_all(outgoing, ('ga', 'dev'), split_axis=1, concat_axis=1, tile...  11.2 us
  transfers between devices with their start and end apart: 4, of which 2 were waited for; matrix products, arithmetic and copies ran while one was open for 6% of the time, Pallas kernels for 0%

commit v1 on v0

v1 whole, which is shorter than its diff:
```python
import functools

import jax
import jax.numpy as jnp
from jax import lax
from jax.experimental import pallas as pl
from jax.experimental.pallas import tpu as pltpu
from jax.sharding import PartitionSpec as P

SUB = 2
DIFFUSION = 0.15
X_DIFFUSION = 0.2
RELAX_RATE = 0.2
LATENT_HEAT = 0.8
STEP_WEIGHT = 0.5
LANES = 128


def mixed(rows, m, keep, levels):
    up = pltpu.roll(rows, rows.shape[0] - 1, 0)
    down = pltpu.roll(rows, 1, 0)
    z = lax.broadcasted_iota(jnp.int32, rows.shape, 0)
    up = jnp.where(z == levels - 1, rows, up)
    down = jnp.where(z == 0, rows, down)
    return keep * rows + m * (up + down)


def crm_kernel(levels, cells, feat_ref, cloudy_ref, theta_ref, water_ref,
               theta_out, water_out, means_out, th, wa, coef, esum):
    zp = feat_ref.shape[1] // 4
    groups = cells // 8
    fields = jnp.transpose(feat_ref[...], (1, 0))
    u, v, heat, wet = (fields[i * zp:(i + 1) * zp] for i in range(4))
    keep_x = 1.0 - 2.0 * X_DIFFUSION
    a = 0.15 * jnp.tanh(u)
    m = 0.1 + 0.15 * jax.nn.sigmoid(v)
    keep = 1.0 - 2.0 * m
    coef[0] = (X_DIFFUSION - a) / keep_x
    coef[1] = (X_DIFFUSION + a) / keep_x
    coef[2] = keep_x * m
    coef[3] = keep_x * keep
    flag = 0.5 * cloudy_ref[0:1].astype(jnp.float32)
    flag8 = jnp.broadcast_to(flag, (8, LANES))

    def widen(z, _):
        for src, dst, slot in ((theta_ref, th, 0), (water_ref, wa, 1)):
            g = src[z].astype(jnp.float32)
            dst[pl.ds(z * cells, cells), :] = g
            s = g[0:8]
            for k in range(1, groups):
                s = s + g[8 * k:8 * k + 8]
            esum[slot, pl.ds(z, 1), :] = jnp.sum(s, axis=0, keepdims=True)
        return 0
    lax.fori_loop(0, levels, widen, 0, unroll=2)

    inv = 1.0 / cells
    mean_t = esum[0] * inv
    mean_w = esum[1] * inv
    condensed = None

    def load_first(ref, z):
        return [ref[pl.ds(z * cells + k, 8, stride=groups), :] for k in range(groups)]

    def load_next(ref, z):
        return [ref[pl.ds(z * cells + 8 * k, 8), :] for k in range(groups)]

    def row(i, z):
        return jnp.broadcast_to(coef[i, pl.ds(z, 1), :], (8, LANES))

    for step in range(SUB):
        last = step == SUB - 1
        mean_t = mixed(mean_t, m, keep, levels)
        mean_w = mixed(mean_w, m, keep, levels)
        relax_t = RELAX_RATE * (heat - mean_t)
        relax_w = RELAX_RATE * (wet - mean_w)
        coef[4] = relax_t
        coef[5] = relax_w
        coef[6] = relax_w - 0.5 * relax_t - 0.5
        load = load_first if step == 0 else load_next

        def advected(z):
            east_c, west_c = row(0, z), row(1, z)
            out = []
            for ref in (th, wa):
                g = load(ref, z)
                east = g[1:] + [pltpu.roll(g[0], 7, 0)]
                west = [pltpu.roll(g[-1], 1, 0)] + g[:-1]
                out.append([g[k] + (east_c * east[k] + west_c * west[k]) for k in range(groups)])
            return out

        def body(z, carry):
            below, here = carry
            above = advected(jnp.minimum(z + 1, levels - 1))
            mz, kz = row(2, z), row(3, z)
            rt, rw, c = row(4, z), row(5, z), row(6, z)
            total = None
            for k in range(groups):
                t = kz * here[0][k] + mz * (above[0][k] + below[0][k])
                w = kz * here[1][k] + mz * (above[1][k] + below[1][k])
                e = flag8 * jnp.maximum((w - 0.5 * t) + c, 0.0)
                t = (t + rt) + LATENT_HEAT * e
                w = (w + rw) - e
                total = e if total is None else total + e
                if last:
                    th[pl.ds(z * cells + k, 8, stride=groups), :] = t
                    wa[pl.ds(z * cells + k, 8, stride=groups), :] = w
                else:
                    th[pl.ds(z * cells + 8 * k, 8), :] = t
                    wa[pl.ds(z * cells + 8 * k, 8), :] = w
            esum[step, pl.ds(z, 1), :] = jnp.sum(total, axis=0, keepdims=True)
            return here, above

        first = advected(0)
        lax.fori_loop(0, levels, body, (first, first), unroll=2)
        excess = esum[step] * inv
        mean_t = mean_t + relax_t + LATENT_HEAT * excess
        mean_w = mean_w + relax_w - excess
        condensed = excess if condensed is None else condensed + excess

    def narrow(z, _):
        theta_out[z] = th[pl.ds(z * cells, cells), :].astype(theta_out.dtype)
        water_out[z] = wa[pl.ds(z * cells, cells), :].astype(water_out.dtype)
        return 0
    lax.fori_loop(0, levels, narrow, 0, unroll=2)
    means_out[...] = jnp.transpose(jnp.concatenate([mean_t, mean_w, condensed, condensed], axis=0), (1, 0))


def crm(feat, cloudy, theta, water):
    levels, cells, slots = theta.shape
    zp = feat.shape[1] // 4
    blk = pl.BlockSpec((levels, cells, LANES), lambda i: (0, 0, i))
    return pl.pallas_call(
        functools.partial(crm_kernel, levels, cells),
        grid=(slots // LANES,),
        out_shape=(jax.ShapeDtypeStruct(theta.shape, theta.dtype),
                   jax.ShapeDtypeStruct(water.shape, water.dtype),
                   jax.ShapeDtypeStruct((slots, 4 * zp), jnp.float32)),
        in_specs=[pl.BlockSpec((LANES, 4 * zp), lambda i: (i, 0)),
                  pl.BlockSpec((1, LANES), lambda i: (0, i)), blk, blk],
        out_specs=(blk, blk, pl.BlockSpec((LANES, 4 * zp), lambda i: (i, 0))),
        scratch_shapes=[pltpu.VMEM((levels * cells, LANES), jnp.float32),
                        pltpu.VMEM((levels * cells, LANES), jnp.float32),
                        pltpu.VMEM((7, zp, LANES), jnp.float32),
                        pltpu.VMEM((2, zp, LANES), jnp.float32)],
        name="crm",
    )(feat, cloudy.reshape(1, slots), theta, water)


def dot(a, b, dims=(((1,), (0,)), ((), ()))):
    return lax.dot_general(a, b, dims, precision=lax.Precision.HIGHEST, preferred_element_type=jnp.float32)


def on_device(column_state, neighbours, crm_slot, cloudy, crm_theta, crm_water):
    fields, levels, columns = column_state.shape
    elements = columns // 4
    devices = lax.axis_size(("ga", "dev"))
    crm_levels = crm_theta.shape[0]
    zp = 64
    state = column_state.reshape(fields * levels, columns)
    member = (jnp.arange(columns)[:, None] // 4 == jnp.arange(elements)[None, :]).astype(jnp.float32)
    mean = dot(state, 0.25 * member)
    forward = [(i, (i + 1) % devices) for i in range(devices)]
    backward = [(b, a) for a, b in forward]
    low = lax.ppermute(mean, ("ga", "dev"), forward)
    high = lax.ppermute(mean, ("ga", "dev"), backward)
    padded = jnp.concatenate([low, mean, high], axis=1)
    offset = lax.axis_index(("ga", "dev")) * elements
    relative = (neighbours - offset + elements) % (elements * devices)
    count = jnp.sum((relative.T[None] == jnp.arange(3 * elements)[:, None, None]).astype(jnp.float32), axis=1)
    laplace = dot(padded, count) - 4.0 * mean
    dynamics = state + DIFFUSION * dot(laplace, member, (((1,), (1,)), ((), ())))
    per_peer = columns // devices
    dest_row = crm_slot // columns * per_peer + crm_slot % per_peer
    place = (dest_row[None, :] == jnp.arange(columns)[:, None]).astype(jnp.float32)
    grid = dynamics.reshape(fields, levels, columns)
    wet = grid[3] + grid[4] + grid[5]
    sent = jnp.concatenate([grid[:3], wet[None]])[:, :crm_levels]
    sent = jnp.pad(sent, ((0, 0), (0, zp - crm_levels), (0, 0))).reshape(4 * zp, columns)
    outgoing = dot(place, sent, (((1,), (1,)), ((), ())))
    arrived = lax.all_to_all(outgoing.reshape(devices, per_peer, 4 * zp), ("ga", "dev"), 0, 0, tiled=True)
    new_theta, new_water, means = crm(arrived.reshape(columns, 4 * zp), cloudy, crm_theta, crm_water)
    back = lax.all_to_all(means[:, :3 * zp].reshape(devices, per_peer, 3 * zp), ("ga", "dev"), 0, 0, tiled=True)
    after = dot(back.reshape(columns, 3 * zp), place, (((0,), (0,)), ((), ()))).reshape(3, zp, columns)[:, :crm_levels]
    low_part = grid[2:5, :crm_levels]
    updated = low_part + STEP_WEIGHT * (after - low_part)
    changed = jnp.concatenate([updated, grid[2:5, crm_levels:]], axis=1)
    new_state = jnp.concatenate([grid[:2], changed, grid[5:]], axis=0)
    return (new_state, new_theta, new_water)


def solution(mesh):
    return jax.shard_map(
        on_device,
        mesh=mesh,
        in_specs=(
            P(None, None, ("ga", "dev")),
            P(("ga", "dev"), None),
            P(("ga", "dev")),
            P(("ga", "dev")),
            P(None, None, ("ga", "dev")),
            P(None, None, ("ga", "dev")),
        ),
        out_specs=(
            P(None, None, ("ga", "dev")),
            P(None, None, ("ga", "dev")),
            P(None, None, ("ga", "dev")),
        ),
        check_vma=False,
    )
```

time: 207 us -> 80.5 us (0.39)
  local copies, waits for them, and re-layouts: 106 us -> 3.73 us
  other arithmetic: 52 us -> 2.63 us
  blocking collectives: 0 us -> 26.6 us
  Pallas kernels: 0 us -> 16.9 us
  starting transfers between devices: 22.5 us -> 7.52 us
  waiting for transfers between devices: 24.8 us -> 17.3 us
  matrix products: 0 us -> 4.77 us
    slice x18 -> x3, local copies, waits for them, and re-layouts: 39 us -> 0.06 us  [the longest x1 0.03 us: on_device(): sent = jnp.concatenate([grid[:3], wet[None]])[:, :crm_levels]]
    scatter-add x1 -> x0, local copies, waits for them, and re-layouts: 36.3 us -> none  [on_device(): dynamics_state.at[2:5, :crm_levels].add(STEP_WEIGHT * column_tendency)]
    all_to_all x0 -> x1, blocking collectives: none -> 26.6 us  [on_device(): lax.all_to_all(outgoing.reshape(devices, per_peer, 4 * zp), ('ga', 'dev')...]
    reduce_sum x4 -> x1, other arithmetic: 20.4 us -> 0.08 us  [on_device(): jnp.sum((relative.T[None] == jnp.arange(3 * elements)[:, None, None]).ast...]
    add x4 -> x2, other arithmetic: 19.8 us -> 0.73 us  [the longest x1 0.69 us: on_device(): dest_row = crm_slot // columns * per_peer + crm_slot % per_peer]
    pallas_call x0 -> x1, Pallas kernels: none -> 16.9 us  [crm(): pl.pallas_call(functools.partial(crm_kernel, levels, cells), grid=(slots...]
    all_to_all x2 -> x1, starting transfers between devices: 19.7 us -> 4.77 us  [on_device(): lax.all_to_all(means[:, :3 * zp].reshape(devices, per_peer, 3 * zp), ('ga...]
    all_to_all x2 -> x1, waiting for transfers between devices: 24.7 us -> 13.4 us  [on_device(): lax.all_to_all(means[:, :3 * zp].reshape(devices, per_peer, 3 * zp), ('ga...]
  transfers between devices with their start and end apart: 4 -> 3, of which waited for: 2 -> 3; matrix products, arithmetic and copies ran while one was open for 6% -> 2% of each run, Pallas kernels for 0% -> 0%
where the time goes in v1:
time: 80.5 us; the launch traced here: 80.2 us
  blocking collectives  26.6 us (33%)
  waiting for transfers between devices  17.3 us (21%)
  Pallas kernels  16.9 us (21%)
  starting transfers between devices  7.52 us (9%)
  matrix products  4.77 us (6%)
  local copies, waits for them, and re-layouts  3.73 us (5%)
  other arithmetic  2.63 us (3%)
    all_to_all x1, blocking collectives, on_device(): lax.all_to_all(outgoing.reshape(devices, per_peer, 4 * zp), ('ga', 'dev')...  26.6 us
    pallas_call x1, Pallas kernels, crm(): pl.pallas_call(functools.partial(crm_kernel, levels, cells), grid=(slots...  16.9 us
    all_to_all x1, waiting for transfers between devices, on_device(): lax.all_to_all(means[:, :3 * zp].reshape(devices, per_peer, 3 * zp), ('ga...  13.4 us
    all_to_all x1, starting transfers between devices, on_device(): lax.all_to_all(means[:, :3 * zp].reshape(devices, per_peer, 3 * zp), ('ga...  4.77 us
    dot_general x5, matrix products, dot(): lax.dot_general(a, b, dims, precision=lax.Precision.HIGHEST, preferred_el...  4.77 us
    ppermute x1, starting transfers between devices, on_device(): low = lax.ppermute(mean, ('ga', 'dev'), forward)  2.74 us
    ppermute x1, waiting for transfers between devices, on_device(): high = lax.ppermute(mean, ('ga', 'dev'), backward)  2.48 us
    reshape x1, local copies, waits for them, and re-layouts, on_device(): means[:, :3 * zp].reshape(devices, per_peer, 3 * zp)  1.98 us
  transfers between devices with their start and end apart: 3, of which 3 were waited for; matrix products, arithmetic and copies ran while one was open for 2% of the time, Pallas kernels for 0%

profile of v1, /device:TPU:1, one launch (start us, length us, event | category | flops | bytes accessed | tf_op | source)
XLA Modules:
  0.0 80.2 jit_solution(11285074914762715219)
XLA Ops:
  0.6 0.0 copy-start
  0.7 2.2 %convolution_bitcast_fusion = f32[432,128]{1,0:T(8,128)S(1)} fusion(f32[432,512]{1,0:T(8,128)} %bitcast.28, s32[512]{0:T(512)S(1)} %add_select_fusion.3), kind=kOutput, calls=%fused_computation.6 | convolution fusion | flops 339869696 | bytes 1107968 | tf_op jit(solution)/shard_map/dot_general | solution.py:150
  2.8 2.7 %collective-permute-start = (f32[432,128]{1,0:T(8,128)S(1)}, f32[432,128]{1,0:T(8,128)S(1)}, u32[]{:S(2)}, u32[]{:S(2)}) collective-permute-start(f32[432,128]{1,0:T(8,128)S(1)} %convolution_bitcast_fusion), channel_id=1, source_target_pairs={{0,1},{1,2},{2,3},{3,4},{4,5},{5,6},{6,7},{7,8},{8,9},{9,10},{10,1... | collective-permute-start | bytes 663560 | tf_op jit(solution)/shard_map/ppermute | solution.py:164
  5.6 0.0 collective-permute-start.1
  5.6 0.7 fusion.25
  6.3 0.1 convert_reduce_fusion
  6.4 0.7 fusion.28
  7.1 1.4 %collective-permute-done = f32[432,128]{1,0:T(8,128)S(1)} collective-permute-done((f32[432,128]{1,0:T(8,128)S(1)}, f32[432,128]{1,0:T(8,128)S(1)}, u32[]{:S(2)}, u32[]{:S(2)}) %collective-permute-start) | collective-permute-done | bytes 221216 | tf_op jit(solution)/shard_map/ppermute | solution.py:164
  8.5 2.5 %collective-permute-done.1 = f32[432,128]{1,0:T(8,128)S(1)} collective-permute-done((f32[432,128]{1,0:T(8,128)S(1)}, f32[432,128]{1,0:T(8,128)S(1)}, u32[]{:S(2)}, u32[]{:S(2)}) %collective-permute-start.1) | collective-permute-done | bytes 221216 | tf_op jit(solution)/shard_map/ppermute | solution.py:165
  10.9 0.7 convolution_subtract_fusion.1
  11.6 0.0 copy-done
  11.7 0.0 copy-start.1
  11.7 0.6 fusion
  12.4 0.0 copy-done.1
  12.4 0.1 fusion.12
  12.5 0.7 fusion.5
  13.2 0.3 copy.15
  13.6 26.6 %all_to_all.10 = f32[128,4,256]{2,1,0:T(4,128)S(1)} all-to-all(f32[128,4,256]{2,1,0:T(4,128)S(1)} %copy.15), channel_id=1, replica_groups=mesh['ga'=4,'dev'=32] {'ga','dev'}, dimensions={0} | all-to-all | bytes 1048576 | tf_op jit(solution)/shard_map/all_to_all | solution.py:180
  40.2 1.0 %reshape.103.feat_ref = f32[512,256]{1,0:T(8,128)} reshape(f32[128,4,256]{2,1,0:T(4,128)S(1)} %all_to_all.10) | data formatting | bytes 1048576 | tf_op jit(solution)/shard_map/reshape | solution.py:181
  41.1 16.9 %crm.1 = (bf16[58,32,512]{2,1,0:T(8,128)(2,1)}, bf16[58,32,512]{2,1,0:T(8,128)(2,1)}, f32[512,256]{1,0:T(8,128)}) custom-call(f32[512,256]{1,0:T(8,128)} %reshape.103.feat_ref, s32[1,512]{1,0:T(1,128)} %bitcast.36, bf16[58,32,512]{2,1,0:T(8,128)(2,1)} %theta_ref.1, bf16[58,32,512]{2,1,0:T(8,128)(2,1)} %water_ref.1), custom_call_target="tpu_custom_call" | custom-call | tf_op jit(solution)/shard_map/crm/pallas_call | solution.py:132
  58.0 2.0 %reshape.105 = f32[128,4,192]{2,1,0:T(4,128)} reshape(f32[512,192]{1,0:T(8,128)} %bitcast.35) | data formatting | bytes 786432 | tf_op jit(solution)/shard_map/reshape | solution.py:182
  60.0 4.8 %all-to-all-start.1 = ((f32[128,4,192]{2,1,0:T(4,128)}), f32[128,4,192]{2,1,0:T(4,128)S(1)}, u32[]{:S(2)}, u32[]{:S(2)}) async-start(f32[128,4,192]{2,1,0:T(4,128)} %reshape.105), calls=%async_computation.1 | async-start | bytes 1048576 | tf_op jit(solution)/shard_map/all_to_all | solution.py:182
  64.8 13.4 %all-to-all-done.1 = f32[128,4,192]{2,1,0:T(4,128)S(1)} async-done(((f32[128,4,192]{2,1,0:T(4,128)}), f32[128,4,192]{2,1,0:T(4,128)S(1)}, u32[]{:S(2)}, u32[]{:S(2)}) %all-to-all-start.1) | async-done | bytes 393248 | tf_op jit(solution)/shard_map/all_to_all | solution.py:182
  78.3 0.2 reshape.106
  78.5 0.2 copy.16
  78.6 0.6 fusion.2
  79.2 1.0 %pad_maximum_fusion = f32[6,72,512]{2,1,0:T(8,128)} fusion(f32[1,72,512]{2,1,0:T(8,128)S(1)} %get-tuple-element.10, f32[3,14,512]{2,1,0:T(8,128)S(1)} %slice.61, f32[3,58,512]{2,1,0:T(8,128)S(1)} %fusion.2, f32[2,72,512]{2,1,0:T(8,128)S(1)} %bitcast.34), kind=kLoop, calls=%fused_computation.11 | loop fusion | flops 663552 | bytes 1769472 | tf_op jit(solution)/shard_map/concatenate | solution.py:187
  (6 shorter events, 0.1 us)
Async XLA Ops:
  0.6 11.0 %copy-start = (f32[6,72,512]{2,1,0:T(8,128)S(1)}, f32[6,72,512]{2,1,0:T(8,128)}, u32[]{:S(2)}) copy-start(f32[6,72,512]{2,1,0:T(8,128)} %param.6) | copy-start | bytes 2654212
  2.8 5.6 %collective-permute-start = (f32[432,128]{1,0:T(8,128)S(1)}, f32[432,128]{1,0:T(8,128)S(1)}, u32[]{:S(2)}, u32[]{:S(2)}) collective-permute-start(f32[432,128]{1,0:T(8,128)S(1)} %convolution_bitcast_fusion), channel_id=1, source_target_pairs={{0,1},{1,2},{2,3},{3,4},{4,5},{5,6},{6,7},{7,8},{8,9},{9,10},{10,1... | collective-permute-start | bytes 663560 | tf_op jit(solution)/shard_map/ppermute | solution.py:164
  5.6 5.4 %collective-permute-start.1 = (f32[432,128]{1,0:T(8,128)S(1)}, f32[432,128]{1,0:T(8,128)S(1)}, u32[]{:S(2)}, u32[]{:S(2)}) collective-permute-start(f32[432,128]{1,0:T(8,128)S(1)} %convolution_bitcast_fusion), channel_id=1, source_target_pairs={{1,0},{2,1},{3,2},{4,3},{5,4},{6,5},{7,6},{8,7},{9,8},{10,9},{11,1... | collective-permute-start | bytes 663560 | tf_op jit(solution)/shard_map/ppermute | solution.py:165
  11.7 0.7 copy-start.1
  60.0 18.3 %all-to-all-start.1 = ((f32[128,4,192]{2,1,0:T(4,128)}), f32[128,4,192]{2,1,0:T(4,128)S(1)}, u32[]{:S(2)}, u32[]{:S(2)}) async-start(f32[128,4,192]{2,1,0:T(4,128)} %reshape.105), calls=%async_computation.1 | async-start | bytes 1048576 | tf_op jit(solution)/shard_map/all_to_all | solution.py:182

commit v2 on v0

v2 whole, which is shorter than its diff:
```python
import functools

import jax
import jax.numpy as jnp
from jax import lax
from jax.experimental import pallas as pl
from jax.experimental.pallas import tpu as pltpu
from jax.sharding import PartitionSpec as P

SUB = 2
DIFFUSION = 0.15
X_DIFFUSION = 0.2
RELAX_RATE = 0.2
LATENT_HEAT = 0.8
STEP_WEIGHT = 0.5
LANES = 128
ROWS = 8
MESH = pl.DeviceIdType.MESH
F32, BF16 = jnp.float32, jnp.bfloat16


def pieces(x):
    high = x.astype(BF16)
    rest = x - high.astype(F32)
    middle = rest.astype(BF16)
    return high, middle, (rest - middle.astype(F32)).astype(BF16)


def dot(a, b, left=1, right=0):
    dims = (((left,), (right,)), ((), ()))
    one = functools.partial(lax.dot_general, dimension_numbers=dims, preferred_element_type=F32)
    if a.dtype == BF16:
        parts = [one(a, p) for p in pieces(b)]
    else:
        parts = [one(p, b) for p in pieces(a)]
    return (parts[2] + parts[1]) + parts[0]


def iota(shape, dim):
    return lax.broadcasted_iota(jnp.int32, shape, dim)


def ones_where(mask, value=1.0):
    return jnp.where(mask, value, 0.0).astype(BF16)


def mixed(rows, m, keep, levels):
    up = pltpu.roll(rows, rows.shape[0] - 1, 0)
    down = pltpu.roll(rows, 1, 0)
    z = iota(rows.shape, 0)
    up = jnp.where(z == levels - 1, rows, up)
    down = jnp.where(z == 0, rows, down)
    return keep * rows + m * (up + down)


def step_kernel(sizes, state_hbm, nb_ref, slot_ref, cloudy_ref, theta_hbm, water_hbm,
                state_out, theta_out, water_out,
                state, mean, low, high, place, theta_in, water_in, th, wa, coef, esum, base,
                fwd_out, fwd_in, ret_out, ret_in,
                load_sem, halo_send, halo_recv, fwd_send, fwd_recv, ret_send, ret_recv):
    planes, per_plane, levels, cells = sizes
    devices = planes * per_plane
    fields, lev, columns = state.shape
    elements = columns // 4
    peer_rows = columns // devices
    zp = coef.shape[1]
    groups = cells // ROWS
    ga, dev = lax.axis_index("ga"), lax.axis_index("dev")
    me = ga * per_plane + dev

    load_state = pltpu.make_async_copy(state_hbm, state, load_sem.at[0])
    load_state.start()
    loads = []
    for b in range(planes):
        for j, (src, dst) in enumerate(((theta_hbm, theta_in), (water_hbm, water_in))):
            loads.append(pltpu.make_async_copy(
                src.at[:, :, pl.ds(b * LANES, LANES)], dst.at[b], load_sem.at[1 + 2 * b + j]))
            loads[-1].start()

    barrier = pltpu.get_barrier_semaphore()

    def greet(k, _):
        p = lax.rem(me + k, devices)
        pl.semaphore_signal(barrier, inc=1, device_id=(p // per_plane, lax.rem(p, per_plane)), device_id_type=MESH)
        return 0
    lax.fori_loop(1, devices, greet, 0)

    load_state.wait()
    flat = state[...].reshape(fields * lev, columns)
    gather = ones_where(iota((columns, elements), 0) // 4 == iota((columns, elements), 1), 0.25)
    mean[...] = dot(flat, gather)
    pl.semaphore_wait(barrier, devices - 1)

    halo = []
    for j, (shift, dst) in enumerate(((1, low), (devices - 1, high))):
        p = lax.rem(me + shift, devices)
        halo.append(pltpu.make_async_remote_copy(
            mean, dst, halo_send.at[j], halo_recv.at[j],
            device_id=(p // per_plane, lax.rem(p, per_plane)), device_id_type=MESH))
        halo[-1].start()

    relative = jnp.bitwise_and(nb_ref[...] - me * elements + elements, elements * devices - 1)

    def counts(part):
        total = None
        for k in range(4):
            hit = jnp.where(relative[k:k + 1] - part * elements == iota((elements, elements), 0), 1.0, 0.0)
            total = hit if total is None else total + hit
        return total.astype(BF16)

    slot = slot_ref[...].reshape(1, columns)
    dest_row = slot // columns * peer_rows + lax.rem(slot, peer_rows)
    place[...] = ones_where(iota((columns, columns), 0) == dest_row)
    own = mean[...]
    laplace = dot(own, counts(1)) - 4.0 * own
    halo[0].wait()
    halo[1].wait()
    laplace = laplace + (dot(low[...], counts(0)) + dot(high[...], counts(2)))
    spread = ones_where(iota((elements, columns), 0) == iota((elements, columns), 1) // 4)
    flat = flat + DIFFUSION * dot(laplace, spread)
    state[...] = flat.reshape(fields, lev, columns)

    kept = [flat[f * lev:f * lev + zp] for f in range(fields)]
    sent = (kept[0], kept[1]), (kept[2], kept[3] + kept[4] + kept[5])
    for h in range(2):
        fwd_out[h] = dot(place[...], jnp.concatenate(sent[h], axis=0), 1, 1)

    def rows_of(ref, p):
        return ref.at[:, pl.ds(pl.multiple_of(p * peer_rows, peer_rows), peer_rows), :]

    own_fwd = pltpu.make_async_copy(rows_of(fwd_out, me), rows_of(fwd_in, me), fwd_recv.at[0])
    own_fwd.start()

    def send_all(k, _):
        turn = k // per_plane
        to_ga = lax.rem(ga + turn, planes)
        to_dev = lax.rem(dev + k, per_plane)
        pltpu.make_async_remote_copy(
            rows_of(fwd_out, to_ga * per_plane + to_dev), rows_of(fwd_in, me), fwd_send, fwd_recv.at[turn],
            device_id=(to_ga, to_dev), device_id_type=MESH).start()
        return 0
    lax.fori_loop(1, devices, send_all, 0)

    inv = 1.0 / cells
    for c in loads:
        c.wait()

    def widen_block(b, _):
        def widen(z, _):
            for j, (src, dst) in enumerate(((theta_in, th), (water_in, wa))):
                g = src[b, z].astype(F32)
                dst[b, pl.ds(z * cells, cells), :] = g
                s = g[0:ROWS]
                for k in range(1, groups):
                    s = s + g[ROWS * k:ROWS * k + ROWS]
                base[b, j, pl.ds(z, 1), :] = jnp.sum(s, axis=0, keepdims=True) * inv
            return 0
        return lax.fori_loop(0, levels, widen, 0, unroll=2)
    lax.fori_loop(0, planes, widen_block, 0)

    def block(turn, _):
        b = lax.rem(ga - turn + planes, planes)
        here_rows = pl.ds(pl.multiple_of(b * LANES, LANES), LANES)
        arrived = fwd_in.at[:, here_rows, :]
        pltpu.make_async_copy(arrived, arrived, fwd_recv.at[turn]).wait()
        wind = jnp.transpose(fwd_in[0, here_rows, :], (1, 0))
        heat_wet = jnp.transpose(fwd_in[1, here_rows, :], (1, 0))
        heat, wet = heat_wet[:zp], heat_wet[zp:]
        keep_x = 1.0 - 2.0 * X_DIFFUSION
        a = 0.15 * jnp.tanh(wind[:zp])
        m = 0.1 + 0.15 * jax.nn.sigmoid(wind[zp:])
        keep = 1.0 - 2.0 * m
        coef[0] = (X_DIFFUSION - a) / keep_x
        coef[1] = (X_DIFFUSION + a) / keep_x
        coef[2] = keep_x * m
        coef[3] = keep_x * keep
        flag = 0.5 * cloudy_ref[here_rows].astype(F32).reshape(1, LANES)
        flag8 = jnp.broadcast_to(flag, (ROWS, LANES))
        mean_t, mean_w = base[b, 0], base[b, 1]
        condensed = None

        def row(i, z):
            return jnp.broadcast_to(coef[i, pl.ds(z, 1), :], (ROWS, LANES))

        for step in range(SUB):
            first, last = step == 0, step == SUB - 1
            mean_t = mixed(mean_t, m, keep, levels)
            mean_w = mixed(mean_w, m, keep, levels)
            relax_t = RELAX_RATE * (heat - mean_t)
            relax_w = RELAX_RATE * (wet - mean_w)
            coef[4] = relax_t
            coef[5] = relax_w
            coef[6] = relax_w - 0.5 * relax_t - 0.5

            def strip(ref, z, k, strided):
                if strided:
                    return ref.at[b, pl.ds(z * cells + k, ROWS, stride=groups), :]
                return ref.at[b, pl.ds(z * cells + ROWS * k, ROWS), :]

            def advected(z):
                east_c, west_c = row(0, z), row(1, z)
                out = []
                for ref in (th, wa):
                    g = [strip(ref, z, k, first)[...] for k in range(groups)]
                    east = g[1:] + [pltpu.roll(g[0], ROWS - 1, 0)]
                    west = [pltpu.roll(g[-1], 1, 0)] + g[:-1]
                    out.append([g[k] + (east_c * east[k] + west_c * west[k]) for k in range(groups)])
                return out

            def body(z, carry):
                below, here = carry
                above = advected(jnp.minimum(z + 1, levels - 1))
                mz, kz = row(2, z), row(3, z)
                rt, rw, c = row(4, z), row(5, z), row(6, z)
                total = None
                for k in range(groups):
                    t = kz * here[0][k] + mz * (above[0][k] + below[0][k])
                    w = kz * here[1][k] + mz * (above[1][k] + below[1][k])
                    e = flag8 * jnp.maximum((w - 0.5 * t) + c, 0.0)
                    total = e if total is None else total + e
                    strip(th, z, k, last)[...] = (t + rt) + LATENT_HEAT * e
                    strip(wa, z, k, last)[...] = (w + rw) - e
                esum[step, pl.ds(z, 1), :] = jnp.sum(total, axis=0, keepdims=True) * inv
                return here, above

            edge = advected(0)
            lax.fori_loop(0, levels, body, (edge, edge), unroll=2)
            excess = esum[step]
            mean_t = mean_t + relax_t + LATENT_HEAT * excess
            mean_w = mean_w + relax_w - excess
            condensed = excess if condensed is None else condensed + excess

        ret_out[0, here_rows, :] = jnp.transpose(jnp.concatenate([mean_t, mean_w], axis=0), (1, 0))
        ret_out[1, here_rows, :] = jnp.transpose(jnp.concatenate([condensed, condensed], axis=0), (1, 0))

        def answer(k, _):
            to_dev = lax.rem(dev + k, per_plane)
            pltpu.make_async_remote_copy(
                rows_of(ret_out, b * per_plane + to_dev), rows_of(ret_in, me), ret_send, ret_recv,
                device_id=(b, to_dev), device_id_type=MESH).start()
            return 0
        lax.fori_loop(jnp.where(turn == 0, 1, 0), per_plane, answer, 0)

        @pl.when(turn == 0)
        def _():
            pltpu.make_async_copy(rows_of(ret_out, me), rows_of(ret_in, me), ret_recv).start()

        def narrow(z, _):
            for src, dst in ((th, theta_out), (wa, water_out)):
                dst[z, :, here_rows] = src[b, pl.ds(z * cells, cells), :].astype(dst.dtype)
            return 0
        lax.fori_loop(0, levels, narrow, 0, unroll=2)
        return 0
    lax.fori_loop(0, planes, block, 0)

    pltpu.make_async_copy(ret_in, ret_in, ret_recv).wait()
    back = [dot(ret_in[h], place[...], 0, 0) for h in range(2)]
    after = {2: back[0][:zp], 3: back[0][zp:], 4: back[1][:zp]}
    state_out[...] = state[...]
    for f, value in after.items():
        old = state[f, :zp, :]
        new = old + STEP_WEIGHT * (value - old)
        state_out[f, :zp, :] = jnp.where(iota((zp, columns), 0) < levels, new, old)

    others = pl.ds(peer_rows, columns - peer_rows)
    for ref, sem in ((fwd_out, fwd_send), (ret_out, ret_send)):
        gone = ref.at[:, others, :]
        pltpu.make_async_copy(gone, gone, sem).wait()


def on_device(planes, per_plane, column_state, neighbours, crm_slot, cloudy, crm_theta, crm_water):
    fields, lev, columns = column_state.shape
    levels, cells, _ = crm_theta.shape
    zp = -(-levels // ROWS) * ROWS
    elements = columns // 4
    blocks = columns // LANES
    wide = pltpu.VMEM((2, columns, 2 * zp), F32)
    halo = pltpu.VMEM((fields * lev, elements), F32)
    narrow_block = pltpu.VMEM((blocks, levels, cells, LANES), crm_theta.dtype)
    wide_block = pltpu.VMEM((blocks, levels * cells, LANES), F32)
    dma = pltpu.SemaphoreType.DMA
    hbm, vmem = pl.BlockSpec(memory_space=pl.ANY), pl.BlockSpec(memory_space=pltpu.VMEM)
    return pl.pallas_call(
        functools.partial(step_kernel, (planes, per_plane, levels, cells)),
        out_shape=tuple(jax.ShapeDtypeStruct(a.shape, a.dtype) for a in (column_state, crm_theta, crm_water)),
        in_specs=[hbm, vmem, vmem, vmem, hbm, hbm],
        out_specs=(vmem, vmem, vmem),
        scratch_shapes=[
            pltpu.VMEM(column_state.shape, F32), halo, halo, halo, pltpu.VMEM((columns, columns), BF16),
            narrow_block, narrow_block, wide_block, wide_block,
            pltpu.VMEM((7, zp, LANES), F32), pltpu.VMEM((SUB, zp, LANES), F32),
            pltpu.VMEM((blocks, 2, zp, LANES), F32),
            wide, wide, wide, wide,
            dma((1 + 2 * blocks,)), dma((2,)), dma((2,)), dma, dma((planes,)), dma, dma,
        ],
        compiler_params=pltpu.CompilerParams(collective_id=0, has_side_effects=True, vmem_limit_bytes=60 * 2 ** 20),
        name="physics_step",
    )(column_state, neighbours.T, crm_slot, cloudy, crm_theta, crm_water)


def solution(mesh):
    split = ("ga", "dev")
    planes, per_plane = mesh.shape["ga"], mesh.shape["dev"]
    return jax.shard_map(
        functools.partial(on_device, planes, per_plane),
        mesh=mesh,
        in_specs=(P(None, None, split), P(split, None), P(split), P(split), P(None, None, split), P(None, None, split)),
        out_specs=(P(None, None, split), P(None, None, split), P(None, None, split)),
        check_vma=False,
    )
```

time: 207 us -> 57.5 us (0.28)
  local copies, waits for them, and re-layouts: 106 us -> 6.53 us
  other arithmetic: 52 us -> 0 us
  Pallas kernels: 0 us -> 50.1 us
  waiting for transfers between devices: 24.8 us -> 0 us
  starting transfers between devices: 22.5 us -> 0 us
    pallas_call x0 -> x1, Pallas kernels: none -> 50.1 us  [on_device(): pl.pallas_call(functools.partial(step_kernel, (planes, per_plane, levels,...]
    slice x18 -> x0, local copies, waits for them, and re-layouts: 39 us -> none  [the longest x6 21.4 us: vertical_mix(): upper_cell = jnp.concatenate([profile[1:], profile[-1:]], axis=0)]
    scatter-add x1 -> x0, local copies, waits for them, and re-layouts: 36.3 us -> none  [on_device(): dynamics_state.at[2:5, :crm_levels].add(STEP_WEIGHT * column_tendency)]
    all_to_all x2 -> x0, waiting for transfers between devices: 24.7 us -> none  [the longest x1 13.5 us: on_device(): lax.all_to_all(flat_tendency, ('ga', 'dev'), split_axis=1, concat_axis=1,...]
    reduce_sum x4 -> x0, other arithmetic: 20.4 us -> none  [the longest x2 19 us: crm_block(): jnp.mean(water_now, axis=1)]
    add x4 -> x0, other arithmetic: 19.8 us -> none  [the longest x2 14.2 us: advect(): profile - 0.5 * advection * (east_side - west_side)]
    all_to_all x2 -> x0, starting transfers between devices: 19.7 us -> none  [the longest x1 14.9 us: on_device(): lax.all_to_all(outgoing, ('ga', 'dev'), split_axis=1, concat_axis=1, tile...]
    gather x6 -> x0, local copies, waits for them, and re-layouts: 8.77 us -> none  [the longest x2 3.77 us: on_device(): outgoing = jnp.take(low_state, send_order, axis=1)]
  transfers between devices with their start and end apart: 4 -> 0, of which waited for: 2 -> 0; matrix products, arithmetic and copies ran while one was open for 6% -> 0% of each run, Pallas kernels for 0% -> 0%
where the time goes in v2:
time: 57.5 us; the launch traced here: 57.3 us
  Pallas kernels  50.1 us (87%)
  local copies, waits for them, and re-layouts  6.53 us (11%)
  between operations  0.64 us (1%)
    pallas_call x1, Pallas kernels, on_device(): pl.pallas_call(functools.partial(step_kernel, (planes, per_plane, levels,...  50.1 us
    unnamed x5, local copies, waits for them, and re-layouts  6.53 us

profile of v2, /device:TPU:1, one launch (start us, length us, event | category | flops | bytes accessed | tf_op | source)
XLA Modules:
  0.0 57.3 jit_solution(7104120457275043927)
XLA Ops:
  0.6 50.1 %physics_step.1 = (f32[6,72,512]{2,1,0:T(8,128)}, bf16[58,32,512]{2,1,0:T(8,128)(2,1)}, bf16[58,32,512]{2,1,0:T(8,128)(2,1)}) custom-call(f32[6,72,512]{2,1,0:T(8,128)} %state_hbm.1, s32[4,128]{1,0:T(4,128)} %bitcast.1, s32[512]{0:T(512)} %slot_ref.1, s32[512]{0:T(512)} %cloudy_ref.1, bf16[58,32,512]{2,1,0:T(8,128)(2,1)} %theta_hbm.1, ...), custom_call_target="tpu_custom_call" | custom-call | tf_op jit(solution)/shard_map/physics_step/pallas_call | solution.py:283
  50.8 2.1 %copy.12 = f32[6,72,512]{2,1,0:T(8,128)} copy(f32[6,72,512]{2,1,0:T(8,128)} %get-tuple-element.6) | data formatting | bytes 1769472
  52.9 0.0 copy-start
  52.9 3.1 %copy.13 = bf16[58,32,512]{2,1,0:T(8,128)(2,1)} copy(bf16[58,32,512]{2,1,0:T(8,128)(2,1)} %get-tuple-element.7) | data formatting | bytes 3801088
  56.0 0.0 copy-done
  56.0 1.2 %copy.14 = bf16[58,32,512]{2,1,0:T(8,128)(2,1)} copy(bf16[58,32,512]{2,1,0:T(8,128)(2,1)S(1)} %copy-done) | data formatting | bytes 3801088
Async XLA Ops:
  52.9 3.1 %copy-start = (bf16[58,32,512]{2,1,0:T(8,128)(2,1)S(1)}, bf16[58,32,512]{2,1,0:T(8,128)(2,1)}, u32[]{:S(2)}) copy-start(bf16[58,32,512]{2,1,0:T(8,128)(2,1)} %get-tuple-element.8) | copy-start | bytes 5701636

commit v3 on v2

--- a/solution.py
+++ b/solution.py
@@ -14,6 +14,7 @@
 LATENT_HEAT = 0.8
 STEP_WEIGHT = 0.5
 LANES = 128
+ORDER = {4: (2, 1, 3, 0)}
 ROWS = 8
 MESH = pl.DeviceIdType.MESH
 F32, BF16 = jnp.float32, jnp.bfloat16
@@ -53,9 +54,9 @@
     return keep * rows + m * (up + down)
 
 
-def step_kernel(sizes, state_hbm, nb_ref, slot_ref, cloudy_ref, theta_hbm, water_hbm,
+def step_kernel(sizes, state_hbm, nb_hbm, slot_hbm, cloudy_hbm, theta_hbm, water_hbm,
                 state_out, theta_out, water_out,
-                state, mean, low, high, place, theta_in, water_in, th, wa, coef, esum, base,
+                nb_ref, slot_ref, cloudy_ref, state, mean, low, high, place, theta_in, water_in, th, wa, coef, esum, base,
                 fwd_out, fwd_in, ret_out, ret_in,
                 load_sem, halo_send, halo_recv, fwd_send, fwd_recv, ret_send, ret_recv):
     planes, per_plane, levels, cells = sizes
@@ -70,6 +71,10 @@
 
     load_state = pltpu.make_async_copy(state_hbm, state, load_sem.at[0])
     load_state.start()
+    small = [pltpu.make_async_copy(src, dst, load_sem.at[1 + 2 * planes + i]) for i, (src, dst) in enumerate(
+        ((nb_hbm, nb_ref), (slot_hbm, slot_ref), (cloudy_hbm, cloudy_ref)))]
+    for c in small:
+        c.start()
     loads = []
     for b in range(planes):
         for j, (src, dst) in enumerate(((theta_hbm, theta_in), (water_hbm, water_in))):
@@ -99,6 +104,8 @@
             device_id=(p // per_plane, lax.rem(p, per_plane)), device_id_type=MESH))
         halo[-1].start()
 
+    for c in small:
+        c.wait()
     relative = jnp.bitwise_and(nb_ref[...] - me * elements + elements, elements * devices - 1)
 
     def counts(part):
@@ -128,18 +135,24 @@
     def rows_of(ref, p):
         return ref.at[:, pl.ds(pl.multiple_of(p * peer_rows, peer_rows), peer_rows), :]
 
-    own_fwd = pltpu.make_async_copy(rows_of(fwd_out, me), rows_of(fwd_in, me), fwd_recv.at[0])
+    own_fwd = pltpu.make_async_copy(rows_of(fwd_out, me), rows_of(fwd_in, me), fwd_recv.at[planes - 1])
     own_fwd.start()
+
+    def ahead(turn):
+        out = (turn * 0)
+        for t, far in enumerate(ORDER[planes]):
+            out = jnp.where(turn == t, far, out)
+        return out
 
     def send_all(k, _):
         turn = k // per_plane
-        to_ga = lax.rem(ga + turn, planes)
-        to_dev = lax.rem(dev + k, per_plane)
+        to_ga = lax.rem(ga - ahead(turn) + planes, planes)
+        to_dev = lax.rem(dev + k + 1, per_plane)
         pltpu.make_async_remote_copy(
             rows_of(fwd_out, to_ga * per_plane + to_dev), rows_of(fwd_in, me), fwd_send, fwd_recv.at[turn],
             device_id=(to_ga, to_dev), device_id_type=MESH).start()
         return 0
-    lax.fori_loop(1, devices, send_all, 0)
+    lax.fori_loop(0, devices - 1, send_all, 0)
 
     inv = 1.0 / cells
     for c in loads:
@@ -159,7 +172,7 @@
     lax.fori_loop(0, planes, widen_block, 0)
 
     def block(turn, _):
-        b = lax.rem(ga - turn + planes, planes)
+        b = lax.rem(ga + ahead(turn), planes)
         here_rows = pl.ds(pl.multiple_of(b * LANES, LANES), LANES)
         arrived = fwd_in.at[:, here_rows, :]
         pltpu.make_async_copy(arrived, arrived, fwd_recv.at[turn]).wait()
@@ -239,9 +252,9 @@
                 rows_of(ret_out, b * per_plane + to_dev), rows_of(ret_in, me), ret_send, ret_recv,
                 device_id=(b, to_dev), device_id_type=MESH).start()
             return 0
-        lax.fori_loop(jnp.where(turn == 0, 1, 0), per_plane, answer, 0)
-
-        @pl.when(turn == 0)
+        lax.fori_loop(jnp.where(turn == planes - 1, 1, 0), per_plane, answer, 0)
+
+        @pl.when(turn == planes - 1)
         def _():
             pltpu.make_async_copy(rows_of(ret_out, me), rows_of(ret_in, me), ret_recv).start()
 
@@ -266,6 +279,15 @@
     for ref, sem in ((fwd_out, fwd_send), (ret_out, ret_send)):
         gone = ref.at[:, others, :]
         pltpu.make_async_copy(gone, gone, sem).wait()
+
+
+def store_kernel(*refs):
+    sems = refs[6]
+    copies = [pltpu.make_async_copy(refs[i], refs[3 + i], sems.at[i]) for i in range(3)]
+    for c in copies:
+        c.start()
+    for c in copies:
+        c.wait()
 
 
 def on_device(planes, per_plane, column_state, neighbours, crm_slot, cloudy, crm_theta, crm_water):
@@ -280,22 +302,34 @@
     wide_block = pltpu.VMEM((blocks, levels * cells, LANES), F32)
     dma = pltpu.SemaphoreType.DMA
     hbm, vmem = pl.BlockSpec(memory_space=pl.ANY), pl.BlockSpec(memory_space=pltpu.VMEM)
-    return pl.pallas_call(
+    inputs = [pltpu.with_memory_space_constraint(a, pltpu.HBM)
+              for a in (column_state, neighbours.T, crm_slot, cloudy, crm_theta, crm_water)]
+    results = pl.pallas_call(
         functools.partial(step_kernel, (planes, per_plane, levels, cells)),
         out_shape=tuple(jax.ShapeDtypeStruct(a.shape, a.dtype) for a in (column_state, crm_theta, crm_water)),
-        in_specs=[hbm, vmem, vmem, vmem, hbm, hbm],
+        in_specs=[hbm] * 6,
         out_specs=(vmem, vmem, vmem),
         scratch_shapes=[
+            pltpu.VMEM((4, elements), jnp.int32), pltpu.VMEM((columns,), jnp.int32), pltpu.VMEM((columns,), jnp.int32),
             pltpu.VMEM(column_state.shape, F32), halo, halo, halo, pltpu.VMEM((columns, columns), BF16),
             narrow_block, narrow_block, wide_block, wide_block,
             pltpu.VMEM((7, zp, LANES), F32), pltpu.VMEM((SUB, zp, LANES), F32),
             pltpu.VMEM((blocks, 2, zp, LANES), F32),
             wide, wide, wide, wide,
-            dma((1 + 2 * blocks,)), dma((2,)), dma((2,)), dma, dma((planes,)), dma, dma,
+            dma((4 + 2 * blocks,)), dma((2,)), dma((2,)), dma, dma((planes,)), dma, dma,
         ],
-        compiler_params=pltpu.CompilerParams(collective_id=0, has_side_effects=True, vmem_limit_bytes=60 * 2 ** 20),
+        compiler_params=pltpu.CompilerParams(collective_id=0, has_side_effects=True, vmem_limit_bytes=28 * 2 ** 20),
         name="physics_step",
-    )(column_state, neighbours.T, crm_slot, cloudy, crm_theta, crm_water)
+    )(*inputs)
+    return pl.pallas_call(
+        store_kernel,
+        out_shape=tuple(jax.ShapeDtypeStruct(a.shape, a.dtype) for a in results),
+        in_specs=[vmem] * 3,
+        out_specs=(hbm, hbm, hbm),
+        scratch_shapes=[dma((3,))],
+        compiler_params=pltpu.CompilerParams(vmem_limit_bytes=16 * 2 ** 20),
+        name="store",
+    )(*results)
 
 
 def solution(mesh):

time: 57.5 us -> 49.8 us (0.87)
  local copies, waits for them, and re-layouts: 6.53 us -> 0 us
  Pallas kernels: 50.1 us -> 49 us
    unnamed x5 -> x0, local copies, waits for them, and re-layouts: 6.53 us -> none
    pallas_call x1, Pallas kernels: 50.1 us -> 46.8 us  [on_device(): pl.pallas_call(functools.partial(step_kernel, (planes, per_plane, levels,...]
    pallas_call x0 -> x1, Pallas kernels: none -> 2.19 us  [on_device(): pl.pallas_call(store_kernel, out_shape=tuple((jax.ShapeDtypeStruct(a.shap...]
where the time goes in v3:
time: 49.8 us; the launch traced here: 49.7 us
  Pallas kernels  49 us (98%)
  between operations  0.64 us (1%)
    pallas_call x1, Pallas kernels, on_device(): pl.pallas_call(functools.partial(step_kernel, (planes, per_plane, levels,...  46.8 us
    pallas_call x1, Pallas kernels, on_device(): pl.pallas_call(store_kernel, out_shape=tuple((jax.ShapeDtypeStruct(a.shap...  2.19 us

profile of v3, /device:TPU:1, one launch (start us, length us, event | category | flops | bytes accessed | tf_op | source)
XLA Modules:
  0.0 49.7 jit_solution(10583825683131406661)
XLA Ops:
  0.6 46.8 %physics_step.1 = (f32[6,72,512]{2,1,0:T(8,128)S(1)}, bf16[58,32,512]{2,1,0:T(8,128)(2,1)S(1)}, bf16[58,32,512]{2,1,0:T(8,128)(2,1)S(1)}) custom-call(f32[6,72,512]{2,1,0:T(8,128)} %state_hbm.1, s32[4,128]{1,0:T(4,128)} %bitcast.1, s32[512]{0:T(512)} %slot_hbm.1, s32[512]{0:T(512)} %cloudy_hbm.1, bf16[58,32,512]{2,1,0:T(8,128)(2,1)} %theta_hbm.1, ...), custom_call_target="tpu_custom_call" | custom-call | tf_op jit(solution)/shard_map/physics_step/pallas_call | solution.py:307
  47.5 2.2 %store.1 = (f32[6,72,512]{2,1,0:T(8,128)}, bf16[58,32,512]{2,1,0:T(8,128)(2,1)}, bf16[58,32,512]{2,1,0:T(8,128)(2,1)}) custom-call(f32[6,72,512]{2,1,0:T(8,128)S(1)} %get-tuple-element.6.refs_0_, bf16[58,32,512]{2,1,0:T(8,128)(2,1)S(1)} %get-tuple-element.7.refs_1_, bf16[58,32,512]{2,1,0:T(8,128)(2,1)S(1)} %get-tuple-element.8.refs_2_), custom_call_target="tpu_custom_call" | custom-call | tf_op jit(solution)/shard_map/store/pallas_call | solution.py:324

commit v4 on v3

--- a/solution.py
+++ b/solution.py
@@ -22,9 +22,7 @@
 
 def pieces(x):
     high = x.astype(BF16)
-    rest = x - high.astype(F32)
-    middle = rest.astype(BF16)
-    return high, middle, (rest - middle.astype(F32)).astype(BF16)
+    return high, (x - high.astype(F32)).astype(BF16)
 
 
 def dot(a, b, left=1, right=0):
@@ -34,7 +32,7 @@
         parts = [one(a, p) for p in pieces(b)]
     else:
         parts = [one(p, b) for p in pieces(a)]
-    return (parts[2] + parts[1]) + parts[0]
+    return parts[1] + parts[0]
 
 
 def iota(shape, dim):
@@ -43,6 +41,12 @@
 
 def ones_where(mask, value=1.0):
     return jnp.where(mask, value, 0.0).astype(BF16)
+
+
+def neighbours_of(g):
+    east = g[1:] + [pltpu.roll(g[0], ROWS - 1, 0)]
+    west = [pltpu.roll(g[-1], 1, 0)] + g[:-1]
+    return east, west
 
 
 def mixed(rows, m, keep, levels):
@@ -56,7 +60,7 @@
 
 def step_kernel(sizes, state_hbm, nb_hbm, slot_hbm, cloudy_hbm, theta_hbm, water_hbm,
                 state_out, theta_out, water_out,
-                nb_ref, slot_ref, cloudy_ref, state, mean, low, high, place, theta_in, water_in, th, wa, coef, esum, base,
+                nb_ref, slot_ref, cloudy_ref, state, mean, low, high, place, theta_in, water_in, even_t, odd_t, even_p, odd_p, coef, sums,
                 fwd_out, fwd_in, ret_out, ret_in,
                 load_sem, halo_send, halo_recv, fwd_send, fwd_recv, ret_send, ret_recv):
     planes, per_plane, levels, cells = sizes
@@ -68,6 +72,8 @@
     groups = cells // ROWS
     ga, dev = lax.axis_index("ga"), lax.axis_index("dev")
     me = ga * per_plane + dev
+    keep_x = 1.0 - 2.0 * X_DIFFUSION
+    side = X_DIFFUSION / keep_x
 
     load_state = pltpu.make_async_copy(state_hbm, state, load_sem.at[0])
     load_state.start()
@@ -84,11 +90,13 @@
 
     barrier = pltpu.get_barrier_semaphore()
 
-    def greet(k, _):
-        p = lax.rem(me + k, devices)
-        pl.semaphore_signal(barrier, inc=1, device_id=(p // per_plane, lax.rem(p, per_plane)), device_id_type=MESH)
-        return 0
-    lax.fori_loop(1, devices, greet, 0)
+    for far in ORDER[planes]:
+        to_ga = lax.rem(ga + far, planes)
+
+        def greet(k, _):
+            pl.semaphore_signal(barrier, inc=1, device_id=(to_ga, jnp.bitwise_xor(dev, k)), device_id_type=MESH)
+            return 0
+        lax.fori_loop(0 if far else 1, per_plane, greet, 0)
 
     load_state.wait()
     flat = state[...].reshape(fields * lev, columns)
@@ -120,6 +128,40 @@
     place[...] = ones_where(iota((columns, columns), 0) == dest_row)
     own = mean[...]
     laplace = dot(own, counts(1)) - 4.0 * own
+    inv = 1.0 / cells
+    for c in loads:
+        c.wait()
+
+    def widen(i, _):
+        b, pair = i // (levels // 2), lax.rem(i, levels // 2)
+        for j in range(2):
+            z = 2 * pair + j
+            half = 0.5 * theta_in[b, z].astype(F32)
+            gap = (water_in[b, z].astype(F32) - half) - 0.5
+            for part, (dst, g) in enumerate(((even_t, half), (even_p, gap))):
+                dst[b, pl.ds(z * cells, cells), :] = g
+                sums[part, b, pl.ds(z * ROWS, ROWS), :] = functools.reduce(
+                    jnp.add, [g[ROWS * k:ROWS * k + ROWS] for k in range(groups)])
+        return 0
+    lax.fori_loop(0, planes * levels // 2, widen, 0)
+
+    def slopes(i, _):
+        b, pair = i // (levels // 2), lax.rem(i, levels // 2)
+        for j in range(2):
+            z = 2 * pair + j
+            for even, odd in ((even_t, odd_t), (even_p, odd_p)):
+                g = [even[b, pl.ds(z * cells + k, ROWS, stride=groups), :] for k in range(groups)]
+                east, west = neighbours_of(g)
+                for k in range(groups):
+                    at = pl.ds(z * cells + ROWS * k, ROWS)
+                    even[b, at, :] = g[k] + side * (east[k] + west[k])
+                    odd[b, at, :] = east[k] - west[k]
+        return 0
+
+    def total_of(part, b):
+        rows = [sums[part, b, pl.ds(k, zp, stride=ROWS), :] for k in range(ROWS)]
+        return functools.reduce(jnp.add, rows) * inv
+
     halo[0].wait()
     halo[1].wait()
     laplace = laplace + (dot(low[...], counts(0)) + dot(high[...], counts(2)))
@@ -144,32 +186,18 @@
             out = jnp.where(turn == t, far, out)
         return out
 
-    def send_all(k, _):
-        turn = k // per_plane
-        to_ga = lax.rem(ga - ahead(turn) + planes, planes)
-        to_dev = lax.rem(dev + k + 1, per_plane)
-        pltpu.make_async_remote_copy(
-            rows_of(fwd_out, to_ga * per_plane + to_dev), rows_of(fwd_in, me), fwd_send, fwd_recv.at[turn],
-            device_id=(to_ga, to_dev), device_id_type=MESH).start()
-        return 0
-    lax.fori_loop(0, devices - 1, send_all, 0)
-
-    inv = 1.0 / cells
-    for c in loads:
-        c.wait()
-
-    def widen_block(b, _):
-        def widen(z, _):
-            for j, (src, dst) in enumerate(((theta_in, th), (water_in, wa))):
-                g = src[b, z].astype(F32)
-                dst[b, pl.ds(z * cells, cells), :] = g
-                s = g[0:ROWS]
-                for k in range(1, groups):
-                    s = s + g[ROWS * k:ROWS * k + ROWS]
-                base[b, j, pl.ds(z, 1), :] = jnp.sum(s, axis=0, keepdims=True) * inv
+    for turn, far in enumerate(ORDER[planes]):
+        to_ga = lax.rem(ga + (planes - far), planes)
+
+        def send(k, _):
+            to_dev = jnp.bitwise_xor(dev, k)
+            pltpu.make_async_remote_copy(
+                rows_of(fwd_out, to_ga * per_plane + to_dev), rows_of(fwd_in, me), fwd_send, fwd_recv.at[turn],
+                device_id=(to_ga, to_dev), device_id_type=MESH).start()
             return 0
-        return lax.fori_loop(0, levels, widen, 0, unroll=2)
-    lax.fori_loop(0, planes, widen_block, 0)
+        lax.fori_loop(0 if far else 1, per_plane, send, 0)
+
+    lax.fori_loop(0, planes * levels // 2, slopes, 0)
 
     def block(turn, _):
         b = lax.rem(ga + ahead(turn), planes)
@@ -179,18 +207,21 @@
         wind = jnp.transpose(fwd_in[0, here_rows, :], (1, 0))
         heat_wet = jnp.transpose(fwd_in[1, here_rows, :], (1, 0))
         heat, wet = heat_wet[:zp], heat_wet[zp:]
-        keep_x = 1.0 - 2.0 * X_DIFFUSION
-        a = 0.15 * jnp.tanh(wind[:zp])
+        slope = (0.15 / keep_x) * jnp.tanh(wind[:zp])
         m = 0.1 + 0.15 * jax.nn.sigmoid(wind[zp:])
         keep = 1.0 - 2.0 * m
-        coef[0] = (X_DIFFUSION - a) / keep_x
-        coef[1] = (X_DIFFUSION + a) / keep_x
-        coef[2] = keep_x * m
-        coef[3] = keep_x * keep
-        flag = 0.5 * cloudy_ref[here_rows].astype(F32).reshape(1, LANES)
-        flag8 = jnp.broadcast_to(flag, (ROWS, LANES))
-        mean_t, mean_w = base[b, 0], base[b, 1]
-        condensed = None
+        coef[0] = slope
+        coef[1] = side - slope
+        coef[2] = side + slope
+        coef[3] = keep_x * m
+        coef[4] = keep_x * keep
+        flag = cloudy_ref[here_rows].astype(F32).reshape(1, LANES)
+        dry = jnp.broadcast_to((0.5 + 0.25 * LATENT_HEAT) * flag, (ROWS, LANES))
+        warm = jnp.broadcast_to((0.25 * LATENT_HEAT) * flag, (ROWS, LANES))
+        mean_t, mean_p = total_of(0, b), total_of(1, b)
+        aim_t = 0.5 * heat
+        aim_p = (wet - aim_t) - 0.5
+        row_t = row_p = condensed = None
 
         def row(i, z):
             return jnp.broadcast_to(coef[i, pl.ds(z, 1), :], (ROWS, LANES))
@@ -198,12 +229,12 @@
         for step in range(SUB):
             first, last = step == 0, step == SUB - 1
             mean_t = mixed(mean_t, m, keep, levels)
-            mean_w = mixed(mean_w, m, keep, levels)
-            relax_t = RELAX_RATE * (heat - mean_t)
-            relax_w = RELAX_RATE * (wet - mean_w)
-            coef[4] = relax_t
-            coef[5] = relax_w
-            coef[6] = relax_w - 0.5 * relax_t - 0.5
+            mean_p = mixed(mean_p, m, keep, levels)
+            relax_t = RELAX_RATE * (aim_t - mean_t)
+            relax_p = RELAX_RATE * (aim_p - mean_p)
+            row_t = relax_t if first else mixed(row_t, m, keep, levels) + relax_t
+            row_p = relax_p if first else mixed(row_p, m, keep, levels) + relax_p
+            coef[5] = row_p
 
             def strip(ref, z, k, strided):
                 if strided:
@@ -211,43 +242,50 @@
                 return ref.at[b, pl.ds(z * cells + ROWS * k, ROWS), :]
 
             def advected(z):
-                east_c, west_c = row(0, z), row(1, z)
+                if first:
+                    rate = row(0, z)
+                    return [[strip(even, z, k, False)[...] - rate * strip(odd, z, k, False)[...] for k in range(groups)]
+                            for even, odd in ((even_t, odd_t), (even_p, odd_p))]
+                east_c, west_c = row(1, z), row(2, z)
                 out = []
-                for ref in (th, wa):
-                    g = [strip(ref, z, k, first)[...] for k in range(groups)]
-                    east = g[1:] + [pltpu.roll(g[0], ROWS - 1, 0)]
-                    west = [pltpu.roll(g[-1], 1, 0)] + g[:-1]
+                for ref in (even_t, even_p):
+                    g = [strip(ref, z, k, False)[...] for k in range(groups)]
+                    east, west = neighbours_of(g)
                     out.append([g[k] + (east_c * east[k] + west_c * west[k]) for k in range(groups)])
                 return out
 
             def body(z, carry):
                 below, here = carry
                 above = advected(jnp.minimum(z + 1, levels - 1))
-                mz, kz = row(2, z), row(3, z)
-                rt, rw, c = row(4, z), row(5, z), row(6, z)
+                mz, kz, offset = row(3, z), row(4, z), row(5, z)
                 total = None
                 for k in range(groups):
                     t = kz * here[0][k] + mz * (above[0][k] + below[0][k])
-                    w = kz * here[1][k] + mz * (above[1][k] + below[1][k])
-                    e = flag8 * jnp.maximum((w - 0.5 * t) + c, 0.0)
+                    p = kz * here[1][k] + mz * (above[1][k] + below[1][k])
+                    e = jnp.maximum(p + offset, 0.0)
                     total = e if total is None else total + e
-                    strip(th, z, k, last)[...] = (t + rt) + LATENT_HEAT * e
-                    strip(wa, z, k, last)[...] = (w + rw) - e
-                esum[step, pl.ds(z, 1), :] = jnp.sum(total, axis=0, keepdims=True) * inv
+                    strip(odd_t if last else even_t, z, k, last)[...] = t + warm * e
+                    strip(odd_p if last else even_p, z, k, last)[...] = p - dry * e
+                sums[step, b, pl.ds(z * ROWS, ROWS), :] = total
                 return here, above
 
             edge = advected(0)
             lax.fori_loop(0, levels, body, (edge, edge), unroll=2)
-            excess = esum[step]
-            mean_t = mean_t + relax_t + LATENT_HEAT * excess
-            mean_w = mean_w + relax_w - excess
+            excess = (0.5 * flag) * total_of(step, b)
+            mean_t = mean_t + relax_t + (0.5 * LATENT_HEAT) * excess
+            mean_p = mean_p + relax_p - (1.0 + 0.5 * LATENT_HEAT) * excess
             condensed = excess if condensed is None else condensed + excess
+
+        coef[5] = row_t + row_t
+        coef[6] = (row_p + row_t) + 0.5
+        mean_w = (mean_p + mean_t) + 0.5
+        mean_t = mean_t + mean_t
 
         ret_out[0, here_rows, :] = jnp.transpose(jnp.concatenate([mean_t, mean_w], axis=0), (1, 0))
         ret_out[1, here_rows, :] = jnp.transpose(jnp.concatenate([condensed, condensed], axis=0), (1, 0))
 
         def answer(k, _):
-            to_dev = lax.rem(dev + k, per_plane)
+            to_dev = jnp.bitwise_xor(dev, k)
             pltpu.make_async_remote_copy(
                 rows_of(ret_out, b * per_plane + to_dev), rows_of(ret_in, me), ret_send, ret_recv,
                 device_id=(b, to_dev), device_id_type=MESH).start()
@@ -259,8 +297,11 @@
             pltpu.make_async_copy(rows_of(ret_out, me), rows_of(ret_in, me), ret_recv).start()
 
         def narrow(z, _):
-            for src, dst in ((th, theta_out), (wa, water_out)):
-                dst[z, :, here_rows] = src[b, pl.ds(z * cells, cells), :].astype(dst.dtype)
+            at = pl.ds(z * cells, cells)
+            half, gap = odd_t[b, at, :], odd_p[b, at, :]
+            add_t, add_w = (jnp.broadcast_to(coef[i, pl.ds(z, 1), :], (cells, LANES)) for i in (5, 6))
+            theta_out[z, :, here_rows] = ((half + half) + add_t).astype(theta_out.dtype)
+            water_out[z, :, here_rows] = ((gap + half) + add_w).astype(water_out.dtype)
             return 0
         lax.fori_loop(0, levels, narrow, 0, unroll=2)
         return 0
@@ -312,13 +353,12 @@
         scratch_shapes=[
             pltpu.VMEM((4, elements), jnp.int32), pltpu.VMEM((columns,), jnp.int32), pltpu.VMEM((columns,), jnp.int32),
             pltpu.VMEM(column_state.shape, F32), halo, halo, halo, pltpu.VMEM((columns, columns), BF16),
-            narrow_block, narrow_block, wide_block, wide_block,
-            pltpu.VMEM((7, zp, LANES), F32), pltpu.VMEM((SUB, zp, LANES), F32),
-            pltpu.VMEM((blocks, 2, zp, LANES), F32),
+            narrow_block, narrow_block, wide_block, wide_block, wide_block, wide_block,
+            pltpu.VMEM((7, zp, LANES), F32), pltpu.VMEM((2, blocks, zp * ROWS, LANES), F32),
             wide, wide, wide, wide,
             dma((4 + 2 * blocks,)), dma((2,)), dma((2,)), dma, dma((planes,)), dma, dma,
         ],
-        compiler_params=pltpu.CompilerParams(collective_id=0, has_side_effects=True, vmem_limit_bytes=28 * 2 ** 20),
+        compiler_params=pltpu.CompilerParams(collective_id=0, has_side_effects=True, vmem_limit_bytes=36 * 2 ** 20),
         name="physics_step",
     )(*inputs)
     return pl.pallas_call(

time: 49.8 us -> 45.4 us (0.912)
  Pallas kernels: 49 us -> 44.7 us
    pallas_call x1, Pallas kernels: 46.8 us -> 42.5 us  [on_device(): pl.pallas_call(functools.partial(step_kernel, (planes, per_plane, levels,...]
where the time goes in v4:
time: 45.4 us; the launch traced here: 45.3 us
  Pallas kernels  44.7 us (98%)
  between operations  0.64 us (1%)
    pallas_call x1, Pallas kernels, on_device(): pl.pallas_call(functools.partial(step_kernel, (planes, per_plane, levels,...  42.5 us
    pallas_call x1, Pallas kernels, on_device(): pl.pallas_call(store_kernel, out_shape=tuple((jax.ShapeDtypeStruct(a.shap...  2.19 us

profile of v4, /device:TPU:1, one launch (start us, length us, event | category | flops | bytes accessed | tf_op | source)
XLA Modules:
  0.0 45.3 jit_solution(12438698666447666108)
XLA Ops:
  0.6 42.5 %physics_step.1 = (f32[6,72,512]{2,1,0:T(8,128)S(1)}, bf16[58,32,512]{2,1,0:T(8,128)(2,1)S(1)}, bf16[58,32,512]{2,1,0:T(8,128)(2,1)S(1)}) custom-call(f32[6,72,512]{2,1,0:T(8,128)} %state_hbm.1, s32[4,128]{1,0:T(4,128)} %bitcast.1, s32[512]{0:T(512)} %slot_hbm.1, s32[512]{0:T(512)} %cloudy_hbm.1, bf16[58,32,512]{2,1,0:T(8,128)(2,1)} %theta_hbm.1, ...), custom_call_target="tpu_custom_call" | custom-call | tf_op jit(solution)/shard_map/physics_step/pallas_call | solution.py:348
  43.1 2.2 %store.1 = (f32[6,72,512]{2,1,0:T(8,128)}, bf16[58,32,512]{2,1,0:T(8,128)(2,1)}, bf16[58,32,512]{2,1,0:T(8,128)(2,1)}) custom-call(f32[6,72,512]{2,1,0:T(8,128)S(1)} %get-tuple-element.6.refs_0_, bf16[58,32,512]{2,1,0:T(8,128)(2,1)S(1)} %get-tuple-element.7.refs_1_, bf16[58,32,512]{2,1,0:T(8,128)(2,1)S(1)} %get-tuple-element.8.refs_2_), custom_call_target="tpu_custom_call" | custom-call | tf_op jit(solution)/shard_map/store/pallas_call | solution.py:364

commit v5 on v4

--- a/solution.py
+++ b/solution.py
@@ -12,6 +12,7 @@
 X_DIFFUSION = 0.2
 RELAX_RATE = 0.2
 LATENT_HEAT = 0.8
+DRYING = 1.0 + 0.5 * LATENT_HEAT
 STEP_WEIGHT = 0.5
 LANES = 128
 ORDER = {4: (2, 1, 3, 0)}
@@ -60,7 +61,7 @@
 
 def step_kernel(sizes, state_hbm, nb_hbm, slot_hbm, cloudy_hbm, theta_hbm, water_hbm,
                 state_out, theta_out, water_out,
-                nb_ref, slot_ref, cloudy_ref, state, mean, low, high, place, theta_in, water_in, even_t, odd_t, even_p, odd_p, coef, sums,
+                nb_ref, slot_ref, cloudy_ref, state, mean, low, high, place, theta_in, water_in, even_p, odd_p, even_c, odd_c, half_way, coef, sums,
                 fwd_out, fwd_in, ret_out, ret_in,
                 load_sem, halo_send, halo_recv, fwd_send, fwd_recv, ret_send, ret_recv):
     planes, per_plane, levels, cells = sizes
@@ -68,7 +69,7 @@
     fields, lev, columns = state.shape
     elements = columns // 4
     peer_rows = columns // devices
-    zp = coef.shape[1]
+    zp = coef.shape[2]
     groups = cells // ROWS
     ga, dev = lax.axis_index("ga"), lax.axis_index("dev")
     me = ga * per_plane + dev
@@ -136,20 +137,20 @@
         b, pair = i // (levels // 2), lax.rem(i, levels // 2)
         for j in range(2):
             z = 2 * pair + j
-            half = 0.5 * theta_in[b, z].astype(F32)
-            gap = (water_in[b, z].astype(F32) - half) - 0.5
-            for part, (dst, g) in enumerate(((even_t, half), (even_p, gap))):
+            warmth, wetness = theta_in[b, z].astype(F32), water_in[b, z].astype(F32)
+            gap = (wetness - 0.5 * warmth) - 0.5
+            for part, (dst, g) in enumerate(((even_p, gap), (even_c, warmth + LATENT_HEAT * wetness))):
                 dst[b, pl.ds(z * cells, cells), :] = g
                 sums[part, b, pl.ds(z * ROWS, ROWS), :] = functools.reduce(
                     jnp.add, [g[ROWS * k:ROWS * k + ROWS] for k in range(groups)])
         return 0
-    lax.fori_loop(0, planes * levels // 2, widen, 0)
+    lax.fori_loop(0, planes * levels // 2, widen, 0, unroll=4)
 
     def slopes(i, _):
         b, pair = i // (levels // 2), lax.rem(i, levels // 2)
         for j in range(2):
             z = 2 * pair + j
-            for even, odd in ((even_t, odd_t), (even_p, odd_p)):
+            for even, odd in ((even_p, odd_p), (even_c, odd_c)):
                 g = [even[b, pl.ds(z * cells + k, ROWS, stride=groups), :] for k in range(groups)]
                 east, west = neighbours_of(g)
                 for k in range(groups):
@@ -197,7 +198,38 @@
             return 0
         lax.fori_loop(0 if far else 1, per_plane, send, 0)
 
-    lax.fori_loop(0, planes * levels // 2, slopes, 0)
+    lax.fori_loop(0, planes * levels // 2, slopes, 0, unroll=4)
+
+    def row(b, i, z):
+        return jnp.broadcast_to(coef[b, i, pl.ds(z, 1), :], (ROWS, LANES))
+
+    def sweep(b, even, odd, store):
+        def strip(ref, z, k):
+            at = pl.ds(z * cells + ROWS * k, ROWS)
+            return ref[at, :] if ref is half_way else ref[b, at, :]
+
+        def advected(z):
+            g = [strip(even, z, k) for k in range(groups)]
+            if odd is not None:
+                rate = row(b, 0, z)
+                return [g[k] - rate * strip(odd, z, k) for k in range(groups)]
+            east_c, west_c = row(b, 1, z), row(b, 2, z)
+            east, west = neighbours_of(g)
+            return [g[k] + (east_c * east[k] + west_c * west[k]) for k in range(groups)]
+
+        def mix(z, below, here, above):
+            mz, kz = row(b, 3, z), row(b, 4, z)
+            store(z, [kz * here[k] + mz * (above[k] + below[k]) for k in range(groups)])
+
+        def body(z, carry):
+            below, here = carry
+            above = advected(z + 1)
+            mix(z, below, here, above)
+            return here, above
+
+        edge = advected(0)
+        below, here = lax.fori_loop(0, levels - 1, body, (edge, edge), unroll=19)
+        mix(levels - 1, below, here, here)
 
     def block(turn, _):
         b = lax.rem(ga + ahead(turn), planes)
@@ -210,76 +242,51 @@
         slope = (0.15 / keep_x) * jnp.tanh(wind[:zp])
         m = 0.1 + 0.15 * jax.nn.sigmoid(wind[zp:])
         keep = 1.0 - 2.0 * m
-        coef[0] = slope
-        coef[1] = side - slope
-        coef[2] = side + slope
-        coef[3] = keep_x * m
-        coef[4] = keep_x * keep
+        for i, rows in enumerate((slope, side - slope, side + slope, keep_x * m, keep_x * keep)):
+            coef[b, i] = rows
         flag = cloudy_ref[here_rows].astype(F32).reshape(1, LANES)
-        dry = jnp.broadcast_to((0.5 + 0.25 * LATENT_HEAT) * flag, (ROWS, LANES))
-        warm = jnp.broadcast_to((0.25 * LATENT_HEAT) * flag, (ROWS, LANES))
-        mean_t, mean_p = total_of(0, b), total_of(1, b)
-        aim_t = 0.5 * heat
-        aim_p = (wet - aim_t) - 0.5
-        row_t = row_p = condensed = None
-
-        def row(i, z):
-            return jnp.broadcast_to(coef[i, pl.ds(z, 1), :], (ROWS, LANES))
+        dry = jnp.broadcast_to((0.5 * DRYING) * flag, (ROWS, LANES))
+        mean_p, mean_c = total_of(0, b), total_of(1, b)
+        aim_p = (wet - 0.5 * heat) - 0.5
+        aim_c = heat + LATENT_HEAT * wet
+        row_p = row_c = condensed = None
 
         for step in range(SUB):
-            first, last = step == 0, step == SUB - 1
-            mean_t = mixed(mean_t, m, keep, levels)
+            first = step == 0
             mean_p = mixed(mean_p, m, keep, levels)
-            relax_t = RELAX_RATE * (aim_t - mean_t)
+            mean_c = mixed(mean_c, m, keep, levels)
             relax_p = RELAX_RATE * (aim_p - mean_p)
-            row_t = relax_t if first else mixed(row_t, m, keep, levels) + relax_t
+            relax_c = RELAX_RATE * (aim_c - mean_c)
             row_p = relax_p if first else mixed(row_p, m, keep, levels) + relax_p
-            coef[5] = row_p
-
-            def strip(ref, z, k, strided):
-                if strided:
-                    return ref.at[b, pl.ds(z * cells + k, ROWS, stride=groups), :]
-                return ref.at[b, pl.ds(z * cells + ROWS * k, ROWS), :]
-
-            def advected(z):
-                if first:
-                    rate = row(0, z)
-                    return [[strip(even, z, k, False)[...] - rate * strip(odd, z, k, False)[...] for k in range(groups)]
-                            for even, odd in ((even_t, odd_t), (even_p, odd_p))]
-                east_c, west_c = row(1, z), row(2, z)
-                out = []
-                for ref in (even_t, even_p):
-                    g = [strip(ref, z, k, False)[...] for k in range(groups)]
-                    east, west = neighbours_of(g)
-                    out.append([g[k] + (east_c * east[k] + west_c * west[k]) for k in range(groups)])
-                return out
-
-            def body(z, carry):
-                below, here = carry
-                above = advected(jnp.minimum(z + 1, levels - 1))
-                mz, kz, offset = row(3, z), row(4, z), row(5, z)
+            row_c = relax_c if first else mixed(row_c, m, keep, levels) + relax_c
+            coef[b, 5] = row_p
+
+            def cloud(z, mixed_cells):
+                offset = row(b, 5, z)
                 total = None
                 for k in range(groups):
-                    t = kz * here[0][k] + mz * (above[0][k] + below[0][k])
-                    p = kz * here[1][k] + mz * (above[1][k] + below[1][k])
-                    e = jnp.maximum(p + offset, 0.0)
+                    e = jnp.maximum(mixed_cells[k] + offset, 0.0)
                     total = e if total is None else total + e
-                    strip(odd_t if last else even_t, z, k, last)[...] = t + warm * e
-                    strip(odd_p if last else even_p, z, k, last)[...] = p - dry * e
-                sums[step, b, pl.ds(z * ROWS, ROWS), :] = total
-                return here, above
-
-            edge = advected(0)
-            lax.fori_loop(0, levels, body, (edge, edge), unroll=2)
-            excess = (0.5 * flag) * total_of(step, b)
-            mean_t = mean_t + relax_t + (0.5 * LATENT_HEAT) * excess
-            mean_p = mean_p + relax_p - (1.0 + 0.5 * LATENT_HEAT) * excess
+                    at = pl.ds(z * cells + ROWS * k, ROWS)
+                    if first:
+                        half_way[at, :] = mixed_cells[k] - dry * e
+                    else:
+                        odd_p[b, at, :] = mixed_cells[k] - dry * e
+                sums[0, b, pl.ds(z * ROWS, ROWS), :] = total
+
+            if first:
+                sweep(b, even_p, odd_p, cloud)
+            else:
+                sweep(b, half_way, None, cloud)
+            excess = (0.5 * flag) * total_of(0, b)
+            mean_p = mean_p + relax_p - DRYING * excess
+            mean_c = mean_c + relax_c
             condensed = excess if condensed is None else condensed + excess
 
-        coef[5] = row_t + row_t
-        coef[6] = (row_p + row_t) + 0.5
-        mean_w = (mean_p + mean_t) + 0.5
-        mean_t = mean_t + mean_t
+        coef[b, 5] = (row_p + (0.5 + 0.5 * row_c)) * (1.0 / DRYING)
+        coef[b, 6] = row_c
+        mean_w = (mean_p + (0.5 + 0.5 * mean_c)) * (1.0 / DRYING)
+        mean_t = mean_c - LATENT_HEAT * mean_w
 
         ret_out[0, here_rows, :] = jnp.transpose(jnp.concatenate([mean_t, mean_w], axis=0), (1, 0))
         ret_out[1, here_rows, :] = jnp.transpose(jnp.concatenate([condensed, condensed], axis=0), (1, 0))
@@ -296,21 +303,39 @@
         def _():
             pltpu.make_async_copy(rows_of(ret_out, me), rows_of(ret_in, me), ret_recv).start()
 
+        return 0
+    lax.fori_loop(0, planes, block, 0)
+
+    def finish(b, _):
+        def keep_cells(z, mixed_cells):
+            for k in range(groups):
+                half_way[pl.ds(z * cells + ROWS * k, ROWS), :] = mixed_cells[k]
+
+        def combine(z, mixed_cells):
+            add_w, add_c = row(b, 5, z), row(b, 6, z)
+            for k in range(groups):
+                gap = odd_p[b, pl.ds(z * cells + ROWS * k, ROWS), :]
+                w = (gap + 0.5 * mixed_cells[k]) * (1.0 / DRYING) + add_w
+                at = pl.ds(z * cells + k, ROWS, stride=groups)
+                even_p[b, at, :] = w
+                odd_c[b, at, :] = (mixed_cells[k] + add_c) - LATENT_HEAT * w
+
+        sweep(b, even_c, odd_c, keep_cells)
+        sweep(b, half_way, None, combine)
+        lanes = pl.ds(pl.multiple_of(b * LANES, LANES), LANES)
+
         def narrow(z, _):
             at = pl.ds(z * cells, cells)
-            half, gap = odd_t[b, at, :], odd_p[b, at, :]
-            add_t, add_w = (jnp.broadcast_to(coef[i, pl.ds(z, 1), :], (cells, LANES)) for i in (5, 6))
-            theta_out[z, :, here_rows] = ((half + half) + add_t).astype(theta_out.dtype)
-            water_out[z, :, here_rows] = ((gap + half) + add_w).astype(water_out.dtype)
+            theta_out[z, :, lanes] = odd_c[b, at, :].astype(theta_out.dtype)
+            water_out[z, :, lanes] = even_p[b, at, :].astype(water_out.dtype)
             return 0
-        lax.fori_loop(0, levels, narrow, 0, unroll=2)
-        return 0
-    lax.fori_loop(0, planes, block, 0)
+        return lax.fori_loop(0, levels, narrow, 0, unroll=29)
+    lax.fori_loop(0, planes, finish, 0)
+    state_out[...] = state[...]
 
     pltpu.make_async_copy(ret_in, ret_in, ret_recv).wait()
     back = [dot(ret_in[h], place[...], 0, 0) for h in range(2)]
     after = {2: back[0][:zp], 3: back[0][zp:], 4: back[1][:zp]}
-    state_out[...] = state[...]
     for f, value in after.items():
         old = state[f, :zp, :]
         new = old + STEP_WEIGHT * (value - old)
@@ -354,7 +379,8 @@
             pltpu.VMEM((4, elements), jnp.int32), pltpu.VMEM((columns,), jnp.int32), pltpu.VMEM((columns,), jnp.int32),
             pltpu.VMEM(column_state.shape, F32), halo, halo, halo, pltpu.VMEM((columns, columns), BF16),
             narrow_block, narrow_block, wide_block, wide_block, wide_block, wide_block,
-            pltpu.VMEM((7, zp, LANES), F32), pltpu.VMEM((2, blocks, zp * ROWS, LANES), F32),
+            pltpu.VMEM((levels * cells, LANES), F32),
+            pltpu.VMEM((blocks, 7, zp, LANES), F32), pltpu.VMEM((2, blocks, zp * ROWS, LANES), F32),
             wide, wide, wide, wide,
             dma((4 + 2 * blocks,)), dma((2,)), dma((2,)), dma, dma((planes,)), dma, dma,
         ],

time: 45.4 us -> 42.4 us (0.934)
  Pallas kernels: 44.7 us -> 41.6 us
    pallas_call x1, Pallas kernels: 42.5 us -> 39.4 us  [on_device(): pl.pallas_call(functools.partial(step_kernel, (planes, per_plane, levels,...]
where the time goes in v5:
time: 42.4 us; the launch traced here: 42.3 us
  Pallas kernels  41.6 us (98%)
  between operations  0.64 us (2%)
    pallas_call x1, Pallas kernels, on_device(): pl.pallas_call(functools.partial(step_kernel, (planes, per_plane, levels,...  39.4 us
    pallas_call x1, Pallas kernels, on_device(): pl.pallas_call(store_kernel, out_shape=tuple((jax.ShapeDtypeStruct(a.shap...  2.19 us

profile of v5, /device:TPU:1, one launch (start us, length us, event | category | flops | bytes accessed | tf_op | source)
XLA Modules:
  0.0 42.3 jit_solution(7320696049602789242)
XLA Ops:
  0.6 39.4 %physics_step.1 = (f32[6,72,512]{2,1,0:T(8,128)S(1)}, bf16[58,32,512]{2,1,0:T(8,128)(2,1)S(1)}, bf16[58,32,512]{2,1,0:T(8,128)(2,1)S(1)}) custom-call(f32[6,72,512]{2,1,0:T(8,128)} %state_hbm.1, s32[4,128]{1,0:T(4,128)} %bitcast.1, s32[512]{0:T(512)} %slot_hbm.1, s32[512]{0:T(512)} %cloudy_hbm.1, bf16[58,32,512]{2,1,0:T(8,128)(2,1)} %theta_hbm.1, ...), custom_call_target="tpu_custom_call" | custom-call | tf_op jit(solution)/shard_map/physics_step/pallas_call | solution.py:373
  40.1 2.2 %store.1 = (f32[6,72,512]{2,1,0:T(8,128)}, bf16[58,32,512]{2,1,0:T(8,128)(2,1)}, bf16[58,32,512]{2,1,0:T(8,128)(2,1)}) custom-call(f32[6,72,512]{2,1,0:T(8,128)S(1)} %get-tuple-element.6.refs_0_, bf16[58,32,512]{2,1,0:T(8,128)(2,1)S(1)} %get-tuple-element.7.refs_1_, bf16[58,32,512]{2,1,0:T(8,128)(2,1)S(1)} %get-tuple-element.8.refs_2_), custom_call_target="tpu_custom_call" | custom-call | tf_op jit(solution)/shard_map/store/pallas_call | solution.py:390

commit v6 on v5

--- a/solution.py
+++ b/solution.py
@@ -16,6 +16,7 @@
 STEP_WEIGHT = 0.5
 LANES = 128
 ORDER = {4: (2, 1, 3, 0)}
+SERVED = {4: (2, 1, 3, 0)}
 ROWS = 8
 MESH = pl.DeviceIdType.MESH
 F32, BF16 = jnp.float32, jnp.bfloat16
@@ -62,8 +63,8 @@
 def step_kernel(sizes, state_hbm, nb_hbm, slot_hbm, cloudy_hbm, theta_hbm, water_hbm,
                 state_out, theta_out, water_out,
                 nb_ref, slot_ref, cloudy_ref, state, mean, low, high, place, theta_in, water_in, even_p, odd_p, even_c, odd_c, half_way, coef, sums,
-                fwd_out, fwd_in, ret_out, ret_in,
-                load_sem, halo_send, halo_recv, fwd_send, fwd_recv, ret_send, ret_recv):
+                pack, start_out, start_in, fwd_out, fwd_in, ret_out, ret_in,
+                load_sem, halo_send, halo_recv, start_send, start_recv, fwd_send, fwd_recv, ret_send, ret_recv):
     planes, per_plane, levels, cells = sizes
     devices = planes * per_plane
     fields, lev, columns = state.shape
@@ -115,6 +116,21 @@
 
     for c in small:
         c.wait()
+    def rows_of(ref, p, count):
+        return ref.at[:, pl.ds(pl.multiple_of(p * count, count), count), :]
+
+    def send_all(src, dst, sent, got, count):
+        for far in ORDER[planes]:
+            to_ga = lax.rem(ga + (planes - far), planes)
+
+            def send(k, _):
+                to_dev = jnp.bitwise_xor(dev, k)
+                pltpu.make_async_remote_copy(
+                    rows_of(src, to_ga * per_plane + to_dev, count), rows_of(dst, me, count), sent, got(far),
+                    device_id=(to_ga, to_dev), device_id_type=MESH).start()
+                return 0
+            lax.fori_loop(0 if far else 1, per_plane, send, 0)
+
     relative = jnp.bitwise_and(nb_ref[...] - me * elements + elements, elements * devices - 1)
 
     def counts(part):
@@ -163,6 +179,11 @@
         rows = [sums[part, b, pl.ds(k, zp, stride=ROWS), :] for k in range(ROWS)]
         return functools.reduce(jnp.add, rows) * inv
 
+    for b in range(planes):
+        total = total_of(1, b)
+        pack[...] = jnp.transpose(jnp.concatenate([total, total], axis=0), (1, 0))
+        evens, odds = pack[pl.ds(0, LANES // 2, stride=2), :], pack[pl.ds(1, LANES // 2, stride=2), :]
+        start_out[0, pl.ds(b * (LANES // 2), LANES // 2), :] = jnp.where(iota(evens.shape, 1) < zp, evens, odds)
     halo[0].wait()
     halo[1].wait()
     laplace = laplace + (dot(low[...], counts(0)) + dot(high[...], counts(2)))
@@ -175,30 +196,23 @@
     for h in range(2):
         fwd_out[h] = dot(place[...], jnp.concatenate(sent[h], axis=0), 1, 1)
 
-    def rows_of(ref, p):
-        return ref.at[:, pl.ds(pl.multiple_of(p * peer_rows, peer_rows), peer_rows), :]
-
-    own_fwd = pltpu.make_async_copy(rows_of(fwd_out, me), rows_of(fwd_in, me), fwd_recv.at[planes - 1])
+    own_fwd = pltpu.make_async_copy(rows_of(fwd_out, me, peer_rows), rows_of(fwd_in, me, peer_rows), fwd_recv.at[0])
     own_fwd.start()
 
     def ahead(turn):
-        out = (turn * 0)
-        for t, far in enumerate(ORDER[planes]):
+        out = turn * 0
+        for t, far in enumerate(SERVED[planes]):
             out = jnp.where(turn == t, far, out)
         return out
 
-    for turn, far in enumerate(ORDER[planes]):
-        to_ga = lax.rem(ga + (planes - far), planes)
-
-        def send(k, _):
-            to_dev = jnp.bitwise_xor(dev, k)
-            pltpu.make_async_remote_copy(
-                rows_of(fwd_out, to_ga * per_plane + to_dev), rows_of(fwd_in, me), fwd_send, fwd_recv.at[turn],
-                device_id=(to_ga, to_dev), device_id_type=MESH).start()
-            return 0
-        lax.fori_loop(0 if far else 1, per_plane, send, 0)
+    send_all(fwd_out, fwd_in, fwd_send, lambda far: fwd_recv.at[far], peer_rows)
 
     lax.fori_loop(0, planes * levels // 2, slopes, 0, unroll=4)
+    own_start = pltpu.make_async_copy(
+        rows_of(start_out, me, peer_rows // 2), rows_of(start_in, me, peer_rows // 2), start_recv)
+    own_start.start()
+    send_all(start_out, start_in, start_send, lambda far: start_recv, peer_rows // 2)
+
 
     def row(b, i, z):
         return jnp.broadcast_to(coef[b, i, pl.ds(z, 1), :], (ROWS, LANES))
@@ -232,10 +246,11 @@
         mix(levels - 1, below, here, here)
 
     def block(turn, _):
-        b = lax.rem(ga + ahead(turn), planes)
+        far = ahead(turn)
+        b = lax.rem(ga + far, planes)
         here_rows = pl.ds(pl.multiple_of(b * LANES, LANES), LANES)
         arrived = fwd_in.at[:, here_rows, :]
-        pltpu.make_async_copy(arrived, arrived, fwd_recv.at[turn]).wait()
+        pltpu.make_async_copy(arrived, arrived, fwd_recv.at[far]).wait()
         wind = jnp.transpose(fwd_in[0, here_rows, :], (1, 0))
         heat_wet = jnp.transpose(fwd_in[1, here_rows, :], (1, 0))
         heat, wet = heat_wet[:zp], heat_wet[zp:]
@@ -246,19 +261,16 @@
             coef[b, i] = rows
         flag = cloudy_ref[here_rows].astype(F32).reshape(1, LANES)
         dry = jnp.broadcast_to((0.5 * DRYING) * flag, (ROWS, LANES))
-        mean_p, mean_c = total_of(0, b), total_of(1, b)
+        mean_p = total_of(0, b)
         aim_p = (wet - 0.5 * heat) - 0.5
-        aim_c = heat + LATENT_HEAT * wet
-        row_p = row_c = condensed = None
+        coef[b, 6] = heat + LATENT_HEAT * wet
+        row_p = condensed = None
 
         for step in range(SUB):
             first = step == 0
             mean_p = mixed(mean_p, m, keep, levels)
-            mean_c = mixed(mean_c, m, keep, levels)
             relax_p = RELAX_RATE * (aim_p - mean_p)
-            relax_c = RELAX_RATE * (aim_c - mean_c)
             row_p = relax_p if first else mixed(row_p, m, keep, levels) + relax_p
-            row_c = relax_c if first else mixed(row_c, m, keep, levels) + relax_c
             coef[b, 5] = row_p
 
             def cloud(z, mixed_cells):
@@ -280,33 +292,39 @@
                 sweep(b, half_way, None, cloud)
             excess = (0.5 * flag) * total_of(0, b)
             mean_p = mean_p + relax_p - DRYING * excess
-            mean_c = mean_c + relax_c
             condensed = excess if condensed is None else condensed + excess
 
-        coef[b, 5] = (row_p + (0.5 + 0.5 * row_c)) * (1.0 / DRYING)
-        coef[b, 6] = row_c
-        mean_w = (mean_p + (0.5 + 0.5 * mean_c)) * (1.0 / DRYING)
-        mean_t = mean_c - LATENT_HEAT * mean_w
-
-        ret_out[0, here_rows, :] = jnp.transpose(jnp.concatenate([mean_t, mean_w], axis=0), (1, 0))
-        ret_out[1, here_rows, :] = jnp.transpose(jnp.concatenate([condensed, condensed], axis=0), (1, 0))
+        ret_out[0, here_rows, :] = jnp.transpose(jnp.concatenate([mean_p, condensed], axis=0), (1, 0))
 
         def answer(k, _):
             to_dev = jnp.bitwise_xor(dev, k)
             pltpu.make_async_remote_copy(
-                rows_of(ret_out, b * per_plane + to_dev), rows_of(ret_in, me), ret_send, ret_recv,
+                rows_of(ret_out, b * per_plane + to_dev, peer_rows), rows_of(ret_in, me, peer_rows), ret_send, ret_recv,
                 device_id=(b, to_dev), device_id_type=MESH).start()
             return 0
-        lax.fori_loop(jnp.where(turn == planes - 1, 1, 0), per_plane, answer, 0)
-
-        @pl.when(turn == planes - 1)
+        lax.fori_loop(jnp.where(far == 0, 1, 0), per_plane, answer, 0)
+
+        @pl.when(far == 0)
         def _():
-            pltpu.make_async_copy(rows_of(ret_out, me), rows_of(ret_in, me), ret_recv).start()
+            pltpu.make_async_copy(rows_of(ret_out, me, peer_rows), rows_of(ret_in, me, peer_rows), ret_recv).start()
 
         return 0
     lax.fori_loop(0, planes, block, 0)
 
+    def relaxed(mean, aim, m, keep):
+        added = None
+        for step in range(SUB):
+            mean = mixed(mean, m, keep, levels)
+            pull = RELAX_RATE * (aim - mean)
+            added = pull if added is None else mixed(added, m, keep, levels) + pull
+            mean = mean + pull
+        return mean, added
+
     def finish(b, _):
+        _, row_c = relaxed(total_of(1, b), coef[b, 6], coef[b, 3] * (1.0 / keep_x), coef[b, 4] * (1.0 / keep_x))
+        coef[b, 5] = (coef[b, 5] + (0.5 + 0.5 * row_c)) * (1.0 / DRYING)
+        coef[b, 6] = row_c
+
         def keep_cells(z, mixed_cells):
             for k in range(groups):
                 half_way[pl.ds(z * cells + ROWS * k, ROWS), :] = mixed_cells[k]
@@ -333,17 +351,25 @@
     lax.fori_loop(0, planes, finish, 0)
     state_out[...] = state[...]
 
+    pltpu.make_async_copy(start_in, start_in, start_recv).wait()
+    source = 2 * iota((columns // 2, columns), 0)
+    first_c = (dot(start_in[0], ones_where(source == dest_row), 0, 0)[:zp]
+               + dot(start_in[0], ones_where(source + 1 == dest_row), 0, 0)[zp:])
+    column_m = 0.1 + 0.15 * jax.nn.sigmoid(state[1, :zp, :])
+    column_wet = (state[3, :zp, :] + state[4, :zp, :]) + state[5, :zp, :]
+    mean_c, _ = relaxed(first_c, state[2, :zp, :] + LATENT_HEAT * column_wet, column_m, 1.0 - 2.0 * column_m)
+
     pltpu.make_async_copy(ret_in, ret_in, ret_recv).wait()
-    back = [dot(ret_in[h], place[...], 0, 0) for h in range(2)]
-    after = {2: back[0][:zp], 3: back[0][zp:], 4: back[1][:zp]}
+    back = dot(ret_in[0], place[...], 0, 0)
+    mean_w = (back[:zp] + (0.5 + 0.5 * mean_c)) * (1.0 / DRYING)
+    after = {2: mean_c - LATENT_HEAT * mean_w, 3: mean_w, 4: back[zp:]}
     for f, value in after.items():
         old = state[f, :zp, :]
         new = old + STEP_WEIGHT * (value - old)
         state_out[f, :zp, :] = jnp.where(iota((zp, columns), 0) < levels, new, old)
 
-    others = pl.ds(peer_rows, columns - peer_rows)
-    for ref, sem in ((fwd_out, fwd_send), (ret_out, ret_send)):
-        gone = ref.at[:, others, :]
+    for ref, sem, count in ((start_out, start_send, peer_rows // 2), (fwd_out, fwd_send, peer_rows), (ret_out, ret_send, peer_rows)):
+        gone = ref.at[:, pl.ds(count, (devices - 1) * count), :]
         pltpu.make_async_copy(gone, gone, sem).wait()
 
 
@@ -362,7 +388,8 @@
     zp = -(-levels // ROWS) * ROWS
     elements = columns // 4
     blocks = columns // LANES
-    wide = pltpu.VMEM((2, columns, 2 * zp), F32)
+    wide, answer = (pltpu.VMEM((n, columns, 2 * zp), F32) for n in (2, 1))
+    start = pltpu.VMEM((1, columns // 2, 2 * zp), F32)
     halo = pltpu.VMEM((fields * lev, elements), F32)
     narrow_block = pltpu.VMEM((blocks, levels, cells, LANES), crm_theta.dtype)
     wide_block = pltpu.VMEM((blocks, levels * cells, LANES), F32)
@@ -381,8 +408,8 @@
             narrow_block, narrow_block, wide_block, wide_block, wide_block, wide_block,
             pltpu.VMEM((levels * cells, LANES), F32),
             pltpu.VMEM((blocks, 7, zp, LANES), F32), pltpu.VMEM((2, blocks, zp * ROWS, LANES), F32),
-            wide, wide, wide, wide,
-            dma((4 + 2 * blocks,)), dma((2,)), dma((2,)), dma, dma((planes,)), dma, dma,
+            pltpu.VMEM((LANES, LANES), F32), start, start, wide, wide, answer, answer,
+            dma((4 + 2 * blocks,)), dma((2,)), dma((2,)), dma, dma, dma, dma((planes,)), dma, dma,
         ],
         compiler_params=pltpu.CompilerParams(collective_id=0, has_side_effects=True, vmem_limit_bytes=36 * 2 ** 20),
         name="physics_step",

time: 42.4 us -> 39.9 us (0.941)
  Pallas kernels: 41.6 us -> 39.2 us
    pallas_call x1, Pallas kernels: 39.4 us -> 37 us  [on_device(): pl.pallas_call(functools.partial(step_kernel, (planes, per_plane, levels,...]
where the time goes in v6:
time: 39.9 us; the launch traced here: 39.8 us
  Pallas kernels  39.2 us (98%)
  between operations  0.64 us (2%)
    pallas_call x1, Pallas kernels, on_device(): pl.pallas_call(functools.partial(step_kernel, (planes, per_plane, levels,...  37 us
    pallas_call x1, Pallas kernels, on_device(): pl.pallas_call(store_kernel, out_shape=tuple((jax.ShapeDtypeStruct(a.shap...  2.19 us

profile of v6, /device:TPU:1, one launch (start us, length us, event | category | flops | bytes accessed | tf_op | source)
XLA Modules:
  0.0 39.8 jit_solution(7400426586057664954)
XLA Ops:
  0.6 37.0 %physics_step.1 = (f32[6,72,512]{2,1,0:T(8,128)S(1)}, bf16[58,32,512]{2,1,0:T(8,128)(2,1)S(1)}, bf16[58,32,512]{2,1,0:T(8,128)(2,1)S(1)}) custom-call(f32[6,72,512]{2,1,0:T(8,128)} %state_hbm.1, s32[4,128]{1,0:T(4,128)} %bitcast.1, s32[512]{0:T(512)} %slot_hbm.1, s32[512]{0:T(512)} %cloudy_hbm.1, bf16[58,32,512]{2,1,0:T(8,128)(2,1)} %theta_hbm.1, ...), custom_call_target="tpu_custom_call" | custom-call | tf_op jit(solution)/shard_map/physics_step/pallas_call | solution.py:400
  37.6 2.2 %store.1 = (f32[6,72,512]{2,1,0:T(8,128)}, bf16[58,32,512]{2,1,0:T(8,128)(2,1)}, bf16[58,32,512]{2,1,0:T(8,128)(2,1)}) custom-call(f32[6,72,512]{2,1,0:T(8,128)S(1)} %get-tuple-element.6.refs_0_, bf16[58,32,512]{2,1,0:T(8,128)(2,1)S(1)} %get-tuple-element.7.refs_1_, bf16[58,32,512]{2,1,0:T(8,128)(2,1)S(1)} %get-tuple-element.8.refs_2_), custom_call_target="tpu_custom_call" | custom-call | tf_op jit(solution)/shard_map/store/pallas_call | solution.py:417

commit v7 on v6

--- a/solution.py
+++ b/solution.py
@@ -62,7 +62,7 @@
 
 def step_kernel(sizes, state_hbm, nb_hbm, slot_hbm, cloudy_hbm, theta_hbm, water_hbm,
                 state_out, theta_out, water_out,
-                nb_ref, slot_ref, cloudy_ref, state, mean, low, high, place, theta_in, water_in, even_p, odd_p, even_c, odd_c, half_way, coef, sums,
+                nb_ref, slot_ref, cloudy_ref, state, mean, low, high, rest_mean, rest_low, rest_high, place, theta_in, water_in, even_p, odd_p, even_c, odd_c, half_way, coef, sums,
                 pack, start_out, start_in, fwd_out, fwd_in, ret_out, ret_in,
                 load_sem, halo_send, halo_recv, start_send, start_recv, fwd_send, fwd_recv, ret_send, ret_recv):
     planes, per_plane, levels, cells = sizes
@@ -101,21 +101,32 @@
         lax.fori_loop(0 if far else 1, per_plane, greet, 0)
 
     load_state.wait()
-    flat = state[...].reshape(fields * lev, columns)
     gather = ones_where(iota((columns, elements), 0) // 4 == iota((columns, elements), 1), 0.25)
-    mean[...] = dot(flat, gather)
+
+    def leading():
+        total = (state[3, :zp, :] + state[4, :zp, :]) + state[5, :zp, :]
+        return jnp.concatenate([state[f, :zp, :] for f in range(3)] + [total], axis=0)
+
+    def trailing():
+        return jnp.concatenate([state[f, zp:, :] for f in range(3)] + [state[f] for f in range(3, fields)], axis=0)
+    mean[...] = dot(leading(), gather)
     pl.semaphore_wait(barrier, devices - 1)
 
-    halo = []
-    for j, (shift, dst) in enumerate(((1, low), (devices - 1, high))):
-        p = lax.rem(me + shift, devices)
-        halo.append(pltpu.make_async_remote_copy(
-            mean, dst, halo_send.at[j], halo_recv.at[j],
-            device_id=(p // per_plane, lax.rem(p, per_plane)), device_id_type=MESH))
-        halo[-1].start()
-
+    def exchange(src, sinks, first):
+        copies = []
+        for j, (shift, dst) in enumerate(zip((1, devices - 1), sinks)):
+            p = lax.rem(me + shift, devices)
+            copies.append(pltpu.make_async_remote_copy(
+                src, dst, halo_send.at[first + j], halo_recv.at[first + j],
+                device_id=(p // per_plane, lax.rem(p, per_plane)), device_id_type=MESH))
+            copies[-1].start()
+        return copies
+    halo = exchange(mean, (low, high), 0)
+    rest_mean[...] = dot(trailing(), gather)
+    rest_halo = exchange(rest_mean, (rest_low, rest_high), 2)
     for c in small:
         c.wait()
+
     def rows_of(ref, p, count):
         return ref.at[:, pl.ds(pl.multiple_of(p * count, count), count), :]
 
@@ -143,8 +154,9 @@
     slot = slot_ref[...].reshape(1, columns)
     dest_row = slot // columns * peer_rows + lax.rem(slot, peer_rows)
     place[...] = ones_where(iota((columns, columns), 0) == dest_row)
+    weights = [counts(part) for part in range(3)]
     own = mean[...]
-    laplace = dot(own, counts(1)) - 4.0 * own
+    laplace = dot(own, weights[1]) - 4.0 * own
     inv = 1.0 / cells
     for c in loads:
         c.wait()
@@ -186,15 +198,11 @@
         start_out[0, pl.ds(b * (LANES // 2), LANES // 2), :] = jnp.where(iota(evens.shape, 1) < zp, evens, odds)
     halo[0].wait()
     halo[1].wait()
-    laplace = laplace + (dot(low[...], counts(0)) + dot(high[...], counts(2)))
+    laplace = laplace + (dot(low[...], weights[0]) + dot(high[...], weights[2]))
     spread = ones_where(iota((elements, columns), 0) == iota((elements, columns), 1) // 4)
-    flat = flat + DIFFUSION * dot(laplace, spread)
-    state[...] = flat.reshape(fields, lev, columns)
-
-    kept = [flat[f * lev:f * lev + zp] for f in range(fields)]
-    sent = (kept[0], kept[1]), (kept[2], kept[3] + kept[4] + kept[5])
+    lead = leading() + DIFFUSION * dot(laplace, spread)
     for h in range(2):
-        fwd_out[h] = dot(place[...], jnp.concatenate(sent[h], axis=0), 1, 1)
+        fwd_out[h] = dot(place[...], lead[2 * zp * h:2 * zp * (h + 1)], 1, 1)
 
     own_fwd = pltpu.make_async_copy(rows_of(fwd_out, me, peer_rows), rows_of(fwd_in, me, peer_rows), fwd_recv.at[0])
     own_fwd.start()
@@ -206,6 +214,9 @@
         return out
 
     send_all(fwd_out, fwd_in, fwd_send, lambda far: fwd_recv.at[far], peer_rows)
+    state_rest = trailing()
+    for f in range(3):
+        state[f, :zp, :] = lead[f * zp:(f + 1) * zp]
 
     lax.fori_loop(0, planes * levels // 2, slopes, 0, unroll=4)
     own_start = pltpu.make_async_copy(
@@ -213,6 +224,16 @@
     own_start.start()
     send_all(start_out, start_in, start_send, lambda far: start_recv, peer_rows // 2)
 
+
+    rest_halo[0].wait()
+    rest_halo[1].wait()
+    own = rest_mean[...]
+    laplace = (dot(own, weights[1]) - 4.0 * own) + (dot(rest_low[...], weights[0]) + dot(rest_high[...], weights[2]))
+    state_rest = state_rest + DIFFUSION * dot(laplace, spread)
+    tops = lev - zp
+    for f in range(3):
+        state[f, zp:, :] = state_rest[f * tops:(f + 1) * tops]
+        state[3 + f] = state_rest[3 * tops + f * lev:3 * tops + (f + 1) * lev]
 
     def row(b, i, z):
         return jnp.broadcast_to(coef[b, i, pl.ds(z, 1), :], (ROWS, LANES))
@@ -390,7 +411,8 @@
     blocks = columns // LANES
     wide, answer = (pltpu.VMEM((n, columns, 2 * zp), F32) for n in (2, 1))
     start = pltpu.VMEM((1, columns // 2, 2 * zp), F32)
-    halo = pltpu.VMEM((fields * lev, elements), F32)
+    halo = pltpu.VMEM((4 * zp, elements), F32)
+    rest = pltpu.VMEM((fields * lev - 3 * zp, elements), F32)
     narrow_block = pltpu.VMEM((blocks, levels, cells, LANES), crm_theta.dtype)
     wide_block = pltpu.VMEM((blocks, levels * cells, LANES), F32)
     dma = pltpu.SemaphoreType.DMA
@@ -404,12 +426,12 @@
         out_specs=(vmem, vmem, vmem),
         scratch_shapes=[
             pltpu.VMEM((4, elements), jnp.int32), pltpu.VMEM((columns,), jnp.int32), pltpu.VMEM((columns,), jnp.int32),
-            pltpu.VMEM(column_state.shape, F32), halo, halo, halo, pltpu.VMEM((columns, columns), BF16),
+            pltpu.VMEM(column_state.shape, F32), halo, halo, halo, rest, rest, rest, pltpu.VMEM((columns, columns), BF16),
             narrow_block, narrow_block, wide_block, wide_block, wide_block, wide_block,
             pltpu.VMEM((levels * cells, LANES), F32),
             pltpu.VMEM((blocks, 7, zp, LANES), F32), pltpu.VMEM((2, blocks, zp * ROWS, LANES), F32),
             pltpu.VMEM((LANES, LANES), F32), start, start, wide, wide, answer, answer,
-            dma((4 + 2 * blocks,)), dma((2,)), dma((2,)), dma, dma, dma, dma((planes,)), dma, dma,
+            dma((4 + 2 * blocks,)), dma((4,)), dma((4,)), dma, dma, dma, dma((planes,)), dma, dma,
         ],
         compiler_params=pltpu.CompilerParams(collective_id=0, has_side_effects=True, vmem_limit_bytes=36 * 2 ** 20),
         name="physics_step",

time: 39.9 us -> 39 us (0.977)
  Pallas kernels: 39.2 us -> 38.2 us
    pallas_call x1, Pallas kernels: 37 us -> 36 us  [on_device(): pl.pallas_call(functools.partial(step_kernel, (planes, per_plane, levels,...]
where the time goes in v7:
time: 39 us; the launch traced here: 38.9 us
  Pallas kernels  38.2 us (98%)
  between operations  0.64 us (2%)
    pallas_call x1, Pallas kernels, on_device(): pl.pallas_call(functools.partial(step_kernel, (planes, per_plane, levels,...  36 us
    pallas_call x1, Pallas kernels, on_device(): pl.pallas_call(store_kernel, out_shape=tuple((jax.ShapeDtypeStruct(a.shap...  2.19 us

profile of v7, /device:TPU:1, one launch (start us, length us, event | category | flops | bytes accessed | tf_op | source)
XLA Modules:
  0.0 38.9 jit_solution(9187264052852499917)
XLA Ops:
  0.6 36.0 %physics_step.1 = (f32[6,72,512]{2,1,0:T(8,128)S(1)}, bf16[58,32,512]{2,1,0:T(8,128)(2,1)S(1)}, bf16[58,32,512]{2,1,0:T(8,128)(2,1)S(1)}) custom-call(f32[6,72,512]{2,1,0:T(8,128)} %state_hbm.1, s32[4,128]{1,0:T(4,128)} %bitcast.1, s32[512]{0:T(512)} %slot_hbm.1, s32[512]{0:T(512)} %cloudy_hbm.1, bf16[58,32,512]{2,1,0:T(8,128)(2,1)} %theta_hbm.1, ...), custom_call_target="tpu_custom_call" | custom-call | tf_op jit(solution)/shard_map/physics_step/pallas_call | solution.py:422
  36.7 2.2 %store.1 = (f32[6,72,512]{2,1,0:T(8,128)}, bf16[58,32,512]{2,1,0:T(8,128)(2,1)}, bf16[58,32,512]{2,1,0:T(8,128)(2,1)}) custom-call(f32[6,72,512]{2,1,0:T(8,128)S(1)} %get-tuple-element.6.refs_0_, bf16[58,32,512]{2,1,0:T(8,128)(2,1)S(1)} %get-tuple-element.7.refs_1_, bf16[58,32,512]{2,1,0:T(8,128)(2,1)S(1)} %get-tuple-element.8.refs_2_), custom_call_target="tpu_custom_call" | custom-call | tf_op jit(solution)/shard_map/store/pallas_call | solution.py:439

commit v8 on v7

--- a/solution.py
+++ b/solution.py
@@ -79,6 +79,16 @@
 
     load_state = pltpu.make_async_copy(state_hbm, state, load_sem.at[0])
     load_state.start()
+    barrier = pltpu.get_barrier_semaphore()
+
+    for far in ORDER[planes]:
+        to_ga = lax.rem(ga + far, planes)
+
+        def greet(k, _):
+            pl.semaphore_signal(barrier, inc=1, device_id=(to_ga, jnp.bitwise_xor(dev, k)), device_id_type=MESH)
+            return 0
+        lax.fori_loop(0 if far else 1, per_plane, greet, 0)
+
     small = [pltpu.make_async_copy(src, dst, load_sem.at[1 + 2 * planes + i]) for i, (src, dst) in enumerate(
         ((nb_hbm, nb_ref), (slot_hbm, slot_ref), (cloudy_hbm, cloudy_ref)))]
     for c in small:
@@ -89,16 +99,6 @@
             loads.append(pltpu.make_async_copy(
                 src.at[:, :, pl.ds(b * LANES, LANES)], dst.at[b], load_sem.at[1 + 2 * b + j]))
             loads[-1].start()
-
-    barrier = pltpu.get_barrier_semaphore()
-
-    for far in ORDER[planes]:
-        to_ga = lax.rem(ga + far, planes)
-
-        def greet(k, _):
-            pl.semaphore_signal(barrier, inc=1, device_id=(to_ga, jnp.bitwise_xor(dev, k)), device_id_type=MESH)
-            return 0
-        lax.fori_loop(0 if far else 1, per_plane, greet, 0)
 
     load_state.wait()
     gather = ones_where(iota((columns, elements), 0) // 4 == iota((columns, elements), 1), 0.25)
@@ -135,12 +135,12 @@
             to_ga = lax.rem(ga + (planes - far), planes)
 
             def send(k, _):
-                to_dev = jnp.bitwise_xor(dev, k)
+                to_dev = jnp.bitwise_xor(dev, per_plane - 1 - k)
                 pltpu.make_async_remote_copy(
                     rows_of(src, to_ga * per_plane + to_dev, count), rows_of(dst, me, count), sent, got(far),
                     device_id=(to_ga, to_dev), device_id_type=MESH).start()
                 return 0
-            lax.fori_loop(0 if far else 1, per_plane, send, 0)
+            lax.fori_loop(0, per_plane if far else per_plane - 1, send, 0)
 
     relative = jnp.bitwise_and(nb_ref[...] - me * elements + elements, elements * devices - 1)
 
@@ -318,12 +318,12 @@
         ret_out[0, here_rows, :] = jnp.transpose(jnp.concatenate([mean_p, condensed], axis=0), (1, 0))
 
         def answer(k, _):
-            to_dev = jnp.bitwise_xor(dev, k)
+            to_dev = jnp.bitwise_xor(dev, per_plane - 1 - k)
             pltpu.make_async_remote_copy(
                 rows_of(ret_out, b * per_plane + to_dev, peer_rows), rows_of(ret_in, me, peer_rows), ret_send, ret_recv,
                 device_id=(b, to_dev), device_id_type=MESH).start()
             return 0
-        lax.fori_loop(jnp.where(far == 0, 1, 0), per_plane, answer, 0)
+        lax.fori_loop(0, jnp.where(far == 0, per_plane - 1, per_plane), answer, 0)
 
         @pl.when(far == 0)
         def _():

time: 39 us -> 37.6 us (0.964)
  Pallas kernels: 38.2 us -> 36.8 us
    pallas_call x1, Pallas kernels: 36 us -> 34.6 us  [on_device(): pl.pallas_call(functools.partial(step_kernel, (planes, per_plane, levels,...]
where the time goes in v8:
time: 37.6 us; the launch traced here: 37.4 us
  Pallas kernels  36.8 us (98%)
  between operations  0.64 us (2%)
    pallas_call x1, Pallas kernels, on_device(): pl.pallas_call(functools.partial(step_kernel, (planes, per_plane, levels,...  34.6 us
    pallas_call x1, Pallas kernels, on_device(): pl.pallas_call(store_kernel, out_shape=tuple((jax.ShapeDtypeStruct(a.shap...  2.19 us

profile of v8, /device:TPU:1, one launch (start us, length us, event | category | flops | bytes accessed | tf_op | source)
XLA Modules:
  0.0 37.4 jit_solution(3761657028759551430)
XLA Ops:
  0.6 34.6 %physics_step.1 = (f32[6,72,512]{2,1,0:T(8,128)S(1)}, bf16[58,32,512]{2,1,0:T(8,128)(2,1)S(1)}, bf16[58,32,512]{2,1,0:T(8,128)(2,1)S(1)}) custom-call(f32[6,72,512]{2,1,0:T(8,128)} %state_hbm.1, s32[4,128]{1,0:T(4,128)} %bitcast.1, s32[512]{0:T(512)} %slot_hbm.1, s32[512]{0:T(512)} %cloudy_hbm.1, bf16[58,32,512]{2,1,0:T(8,128)(2,1)} %theta_hbm.1, ...), custom_call_target="tpu_custom_call" | custom-call | tf_op jit(solution)/shard_map/physics_step/pallas_call | solution.py:422
  35.2 2.2 %store.1 = (f32[6,72,512]{2,1,0:T(8,128)}, bf16[58,32,512]{2,1,0:T(8,128)(2,1)}, bf16[58,32,512]{2,1,0:T(8,128)(2,1)}) custom-call(f32[6,72,512]{2,1,0:T(8,128)S(1)} %get-tuple-element.6.refs_0_, bf16[58,32,512]{2,1,0:T(8,128)(2,1)S(1)} %get-tuple-element.7.refs_1_, bf16[58,32,512]{2,1,0:T(8,128)(2,1)S(1)} %get-tuple-element.8.refs_2_), custom_call_target="tpu_custom_call" | custom-call | tf_op jit(solution)/shard_map/store/pallas_call | solution.py:439
